TPU v7x, 32 devices: a whole 2x2x4 slice. The times are simulated.
32 devices in a mesh: grp: 4 (over y, x), slab: 8 (over z, core).
Axes of the slice: x: 2, y: 2, z: 4, core: 2. Of those that a mesh axis runs over, the one named last changes fastest.
Arguments:
- forcing: float32 [4, 3, 64, 128, 128], P('grp', None, 'slab'), may hold values from -18 to 18
- stiffness: float32 [4, 3, 64, 128, 128], P('grp', None, 'slab'), may hold values from 0.25 to 4
- anisotropy: float32 [4, 3, 3], P('grp'), may hold values from 0.3 to 3
- coupling: float32 [4, 3, 3], P('grp'), may hold values from -0.3 to 2, as said below
- levels: int32 [4, 2], replicated, may hold values from 0 to 2
- neighbours: int32 [4, 3], replicated, may hold values from -1 to 3, as said below
Outputs:
- mixed: float32 [4, 3, 64, 128, 128], P('grp', None, 'slab')
Inputs may be any that keep to these rules, and one draw needn't show every extreme that they name: neighbours[g, 0], [g, 1], [g, 2] name a pair whose levels are those of pair g less (1, 0), (0, 1), (1, 1), or are -1 where no pair has those levels. `coupling`: symmetric; diagonal entries 0.8 to 2, off-diagonal entries at most 0.3 in magnitude.
All inputs are finite; a program needn't handle non-finite values.
Results may differ from a plain program's by a relative error of at most 0.0003.
Values sent between devices are 32-bit elements; how exact they have to be, the bound alone decides.
No kernel may reach another device: no remote copies, remote signals or barrier semaphores. Data moves between devices by JAX's collectives and lax.ppermute only.
A program may use at most 64 MiB of HBM per device.

v0:
```python
import jax
import jax.numpy as jnp
from jax import lax
from jax.sharding import PartitionSpec as P

ITERS = 2


exact_mode = lax.Precision.HIGHEST


def padded_2(shard, sides, width):
    for axis, dim in sides:
        peers, length = (lax.axis_size(axis), shard.shape[dim])
        up = [(i, (i + 1) % peers) for i in range(peers - 1)]
        down = [(j, i) for i, j in up]
        last = lax.slice_in_dim(shard, length - width, length, axis=dim)
        leading = lax.slice_in_dim(shard, 0, width, axis=dim)
        before = lax.ppermute(last, axis, up)
        after = lax.ppermute(leading, axis, down)
        shard = jnp.concatenate([before, shard, after], axis=dim)
    return shard


def level_factor(level_ids):
    return jnp.where(level_ids == 0, 4, jnp.where(level_ids == 1, 2, 1)).astype(jnp.int32)


def pair_shape(levels, pair_ids, width, depth, slabs):
    chosen = jnp.take(levels, pair_ids, axis=0)
    cells_x = width // level_factor(chosen[..., 0])
    run_z = depth // level_factor(chosen[..., 1])
    return (cells_x, run_z, run_z * slabs)


def step_up(values, axis_dim):
    length = values.shape[axis_dim]
    widths = [(0, 0)] * values.ndim
    widths[axis_dim] = (0, 1)
    return lax.slice_in_dim(jnp.pad(values, widths), 1, length + 1, axis=axis_dim)


def step_down(values, axis_dim):
    length = values.shape[axis_dim]
    widths = [(0, 0)] * values.ndim
    widths[axis_dim] = (1, 0)
    return lax.slice_in_dim(jnp.pad(values, widths), 0, length, axis=axis_dim)


def spread_out(totals):
    return totals[:, None, None, None, None]


def with_rims(values, run_z):
    row_index = jnp.arange(values.shape[2], dtype=jnp.int32)
    picking = (row_index[None, :] == run_z[:, None] - 1).astype(jnp.float32)
    last_row = jnp.sum(values * picking[:, None, :, None, None], axis=2)
    stacked = jnp.stack([values[:, :, 0], last_row], axis=2)
    padded = padded_2(stacked, (("slab", 2),), 1)
    return (padded[:, :, 0], padded[:, :, 3])


def z_beside(values, run_z, below_rim, above_rim):
    row_index = jnp.arange(values.shape[2], dtype=jnp.int32)
    above_rows = jnp.concatenate([values[:, :, 1:], jnp.zeros_like(values[:, :, :1])], axis=2)
    at_top = (row_index[None, :] == run_z[:, None] - 1)[:, None, :, None, None]
    above_rows = jnp.where(at_top, above_rim[:, :, None], above_rows)
    below_rows = jnp.concatenate([below_rim[:, :, None], values[:, :, :-1]], axis=2)
    return (above_rows, below_rows)


def operate(values, run_z, face_list, coefficient, coupling, active):
    below_rim, above_rim = with_rims(values, run_z)
    above_rows, below_rows = z_beside(values, run_z, below_rim, above_rim)
    beside = (
        (step_up(values, 4), step_down(values, 4)),
        (step_up(values, 3), step_down(values, 3)),
        (above_rows, below_rows),
    )
    result = jnp.sum(coupling[:, :, :, None, None, None] * values[:, None], axis=2)
    for facing in range(3):
        upper_face, lower_face = face_list[facing]
        result = result + coefficient[:, :, facing, None, None, None] * (
            upper_face * (values - beside[facing][0]) + lower_face * (values - beside[facing][1])
        )
    return result * active


def pair_sums(first, second):
    return jnp.sum(first * second, axis=(1, 2, 3, 4))


def joint_totals(residual, precond, applied):
    return lax.psum((pair_sums(residual, precond), pair_sums(precond, applied)), "slab")


def mixing_weights(levels, neighbours, target, sources, width, depth, slabs, slab_index):
    target_x, target_run, target_depth = pair_shape(levels, target, width, depth, slabs)
    source_x, source_run, source_depth = pair_shape(levels, sources, width, depth, slabs)
    link_ids = jnp.take(neighbours, target, axis=0)
    signs = (
        (sources == target).astype(jnp.float32)
        - (sources == link_ids[0]).astype(jnp.float32)
        - (sources == link_ids[1]).astype(jnp.float32)
        + (sources == link_ids[2]).astype(jnp.float32)
    )
    fine_x = jnp.arange(width, dtype=jnp.int32)
    centres_x = fine_x.astype(jnp.float32) + 0.5
    along_x = (
        centres_x[None, :] * (source_x.astype(jnp.float32) / target_x.astype(jnp.float32))[:, None]
    )
    weight_x = jnp.maximum(0.0, 1.0 - jnp.abs(along_x[:, :, None] - centres_x[None, None, :]))
    weight_x = weight_x * (fine_x < target_x).astype(jnp.float32)[None, :, None]
    weight_x = weight_x * (fine_x[None, :] < source_x[:, None]).astype(jnp.float32)[:, None, :]
    fine_z = jnp.arange(depth, dtype=jnp.int32)
    along_z = ((slab_index * target_run + fine_z).astype(jnp.float32) + 0.5)[None, :] * (
        source_depth.astype(jnp.float32) / target_depth.astype(jnp.float32)
    )[:, None]
    columns = jnp.arange(depth + 2, dtype=jnp.int32)
    coarse_ids = slab_index * source_run[:, None] - 1 + columns[None, :]
    coarse_ids = jnp.where(
        columns[None, :] == depth + 1, (slab_index + 1) * source_run[:, None], coarse_ids
    )
    weight_z = jnp.maximum(
        0.0, 1.0 - jnp.abs(along_z[:, :, None] - (coarse_ids.astype(jnp.float32) + 0.5)[:, None, :])
    )
    weight_z = (
        weight_z * (fine_z < target_run).astype(jnp.float32)[None, :, None] * signs[:, None, None]
    )
    return (weight_x, weight_z)


def contribute(pieces, weight_x, weight_z):
    vertical = jnp.einsum("pkn,pcnyx->pckyx", weight_z, pieces, precision=exact_mode)
    return jnp.einsum("pckyx,pmx->ckym", vertical, weight_x, precision=exact_mode)


def per_device(forcing, stiffness, anisotropy, coupling, levels, neighbours):
    own_count = forcing.shape[0]
    depth = forcing.shape[2]
    height = forcing.shape[3]
    width = forcing.shape[4]
    slabs = lax.axis_size("slab")
    slab_index = lax.axis_index("slab")
    own_ids = lax.axis_index("grp") * own_count + jnp.arange(own_count, dtype=jnp.int32)
    cells_x, run_z, depth_z = pair_shape(levels, own_ids, width, depth, slabs)
    row_index = jnp.arange(depth, dtype=jnp.int32)
    col_index = jnp.arange(width, dtype=jnp.int32)
    active = (
        (row_index[None, :] < run_z[:, None])[:, None, :, None, None]
        & (col_index[None, :] < cells_x[:, None])[:, None, None, None, :]
    ).astype(jnp.float32)
    source = forcing * active
    scales = jnp.stack(
        [
            (cells_x.astype(jnp.float32) / height) ** 2,
            jnp.ones(own_count, jnp.float32),
            (depth_z.astype(jnp.float32) / height) ** 2,
        ],
        axis=1,
    )
    coefficient = anisotropy * scales[:, None, :]
    kept = stiffness * active
    vertical_k = kept[:, 2:3]
    below_k, above_k = with_rims(vertical_k, run_z)
    above_rows_k, below_rows_k = z_beside(vertical_k, run_z, below_k, above_k)
    diagonal = jnp.diagonal(coupling, axis1=1, axis2=2)[:, :, None, None, None]
    face_list = []
    for facing in range(3):
        single = kept[:, facing : facing + 1]
        if facing == 2:
            upper_face = 0.5 * (single + above_rows_k)
            lower_face = 0.5 * (single + below_rows_k)
        else:
            upper_face = 0.5 * (single + step_up(single, 4 - facing))
            lower_face = 0.5 * (single + step_down(single, 4 - facing))
        face_list.append((upper_face, lower_face))
        diagonal = diagonal + coefficient[:, :, facing, None, None, None] * (
            upper_face + lower_face
        )
    solution = jnp.zeros_like(source)
    residual = source
    precond = residual / diagonal
    applied = operate(precond, run_z, face_list, coefficient, coupling, active)
    rz_now, curvature = joint_totals(residual, precond, applied)
    step_size = rz_now / curvature
    search = precond
    along_image = applied
    for iteration in range(ITERS):
        solution = solution + spread_out(step_size) * search
        if iteration + 1 < ITERS:
            residual = residual - spread_out(step_size) * along_image
            precond = residual / diagonal
            applied = operate(precond, run_z, face_list, coefficient, coupling, active)
            rz_next, curvature = joint_totals(residual, precond, applied)
            beta_ratio = rz_next / rz_now
            step_size = rz_next / (curvature - beta_ratio * rz_next / step_size)
            search = precond + spread_out(beta_ratio) * search
            along_image = applied + spread_out(beta_ratio) * along_image
            rz_now = rz_next
    below_rim, above_rim = with_rims(solution, run_z)
    extended = jnp.concatenate([below_rim[:, :, None], solution, above_rim[:, :, None]], axis=2)
    empty = jnp.zeros((own_count, 3, depth, height, width), jnp.float32)
    pieces = lax.all_gather(extended, "grp", axis=0, tiled=True)
    sources = jnp.arange(pieces.shape[0], dtype=jnp.int32)
    weight_x, weight_z = mixing_weights(
        levels, neighbours, own_ids[0], sources, width, depth, slabs, slab_index
    )
    updated = [empty[0] + contribute(pieces, weight_x, weight_z)]
    return jnp.stack(updated)


def solution(mesh):
    return jax.shard_map(
        per_device,
        mesh=mesh,
        in_specs=(
            P("grp", None, "slab", None, None),
            P("grp", None, "slab", None, None),
            P("grp", None, None),
            P("grp", None, None),
            P(),
            P(),
        ),
        out_specs=P("grp", None, "slab", None, None),
        check_vma=False,
    )
```

profile of v0, /device:TPU:1, one launch (start us, length us, event | category | flops | bytes accessed | tf_op | source)
XLA Modules:
  0.0 215.1 jit_solution(7938127954803522138)
XLA Ops:
  6.5 0.8 dynamic-slice_select_fusion
  7.4 0.6 fusion.109
  10.7 0.1 and_convert_fusion
  10.8 1.5 broadcast_multiply_fusion
  12.3 0.0 copy-start.17
  12.3 0.0 copy-start.18
  12.4 0.1 multiply_reduce_fusion.8
  12.5 4.6 %collective-permute-start.1 = (f32[1,1,1,128,128]{4,3,2,1,0:T(8,128)S(1)}, f32[1,1,1,128,128]{4,3,2,1,0:T(8,128)S(1)}, u32[]{:S(2)}, u32[]{:S(2)}) collective-permute-start(f32[1,1,1,128,128]{4,3,2,1,0:T(8,128)S(1)} %bitcast.95), channel_id=1, source_target_pairs={{0,1},{1,2},{2,3},{3,4},{4,5},{5,6},{6,7},{8,9},{9,10},{10,11},{11... | collective-permute-start | bytes 196616 | tf_op jit(solution)/shard_map/ppermute | solution.py:19
  17.1 1.9 collective-permute-start
  19.0 0.1 fusion.108
  19.1 0.1 maximum_bitcast_fusion
  19.2 0.2 slice_reduce_fusion.2
  19.4 0.7 gather_fusion
  20.1 0.0 collective-permute-done.1
  20.1 2.6 %collective-permute-done = f32[1,1,1,128,128]{4,3,2,1,0:T(8,128)S(1)} collective-permute-done((f32[1,1,1,128,128]{4,3,2,1,0:T(8,128)S(1)}, f32[1,1,1,128,128]{4,3,2,1,0:T(8,128)S(1)}, u32[]{:S(2)}, u32[]{:S(2)}) %collective-permute-start) | collective-permute-done | bytes 65568 | tf_op jit(solution)/shard_map/ppermute | solution.py:20
  22.7 0.3 fusion.102
  23.0 0.6 fusion.74
  23.6 0.0 copy-start
  23.6 0.2 fusion.66
  23.8 2.3 %copy-done = f32[1,3,8,128,128]{4,3,2,1,0:T(8,128)S(1)} copy-done((f32[1,3,8,128,128]{4,3,2,1,0:T(8,128)S(1)}, f32[1,3,8,128,128]{4,3,2,1,0:T(8,128)}, u32[]{:S(2)}) %copy-start) | copy-done | bytes 1572888
  26.1 0.6 multiply_reduce_fusion.6
  26.8 0.4 fusion.107
  27.2 1.9 collective-permute-start.2
  29.1 3.6 %collective-permute-start.3 = (f32[1,3,1,128,128]{4,3,2,1,0:T(8,128)S(1)}, f32[1,3,1,128,128]{4,3,2,1,0:T(8,128)S(1)}, u32[]{:S(2)}, u32[]{:S(2)}) collective-permute-start(f32[1,3,1,128,128]{4,3,2,1,0:T(8,128)S(1)} %bitcast.91), channel_id=1, source_target_pairs={{0,1},{1,2},{2,3},{3,4},{4,5},{5,6},{6,7},{8,9},{9,10},{10,11},{11... | collective-permute-start | bytes 589832 | tf_op jit(solution)/shard_map/ppermute | solution.py:19
  32.8 0.4 multiply_reduce_fusion.1
  33.2 1.0 collective-permute-done.2
  34.2 1.2 collective-permute-done.3
  35.4 0.0 copy-done.9
  35.4 3.9 %multiply_reduce_fusion.5 = (f32[]{:T(128)}, f32[]{:T(128)}, f32[1,3,8,128,128]{4,3,2,1,0:T(8,128)}) fusion(f32[1,3,8,128,128]{4,3,2,1,0:T(8,128)S(1)} %get-tuple-element.60, f32[1,3,8,128,128]{4,3,2,1,0:T(8,128)S(1)} %copy-done, f32[8,128]{1,0:T(8,128)S(1)} %and_convert_fusion, f32[1,3,7,128,128]{4,3,2,1,0:T(8,128)S(1)} %get-tuple-element.69, ...), kind=kLoop, calls=%fused_computation.65 | loop fusion | flops 11403262 | bytes 12587060 | tf_op jit(solution)/shard_map/reduce_sum | solution.py:90
  39.3 15.1 %all-reduce.16 = (f32[1]{0:T(128)}, f32[1]{0:T(128)}) all-reduce(f32[1]{0:T(128)} %bitcast.19, f32[1]{0:T(128)} %bitcast.30), channel_id=1, replica_groups=mesh['grp'=4,'slab'=8] {'slab'}, use_global_device_ids=true, to_apply=%region_2.3 | all-reduce | flops 2 | bytes 16 | tf_op jit(solution)/shard_map/psum | solution.py:94
  55.7 3.8 %multiply_reduce_fusion.3 = (f32[3,128,128]{2,1,0:T(8,128)S(1)}, f32[]{:T(128)}, f32[1,3,8,128,128]{4,3,2,1,0:T(8,128)S(1)}) fusion(f32[8]{0:T(128)S(1)} %fusion.101, f32[1,3,8,128,128]{4,3,2,1,0:T(8,128)} %get-tuple-element.58, f32[]{:T(128)} %bitcast.31, f32[1,3,8,128,128]{4,3,2,1,0:T(8,128)} %param.6, f32[8,128]{1,0:T(8,128)S(1)} %and_convert_fusion, ...), kind=kLoop, calls=%fused_computation.62 | loop fusion | flops 5455871 | bytes 6492248 | tf_op jit(solution)/shard_map/reduce_sum | solution.py:57
  59.4 0.4 fusion.106
  59.8 2.1 collective-permute-start.4
  61.9 3.5 %collective-permute-start.5 = (f32[1,3,1,128,128]{4,3,2,1,0:T(8,128)S(1)}, f32[1,3,1,128,128]{4,3,2,1,0:T(8,128)S(1)}, u32[]{:S(2)}, u32[]{:S(2)}) collective-permute-start(f32[1,3,1,128,128]{4,3,2,1,0:T(8,128)S(1)} %bitcast.89), channel_id=1, source_target_pairs={{0,1},{1,2},{2,3},{3,4},{4,5},{5,6},{6,7},{8,9},{9,10},{10,11},{11... | collective-permute-start | bytes 589832 | tf_op jit(solution)/shard_map/ppermute | solution.py:19
  65.5 0.4 multiply_reduce_fusion
  65.9 0.9 collective-permute-done.4
  66.8 1.2 collective-permute-done.5
  68.0 2.7 %fusion.48 = f32[]{:T(128)} fusion(f32[1,3,8,128,128]{4,3,2,1,0:T(8,128)S(1)} %get-tuple-element.57, f32[1,3,7,128,128]{4,3,2,1,0:T(8,128)S(1)} %get-tuple-element.65, f32[1,3,1,128,128]{4,3,2,1,0:T(8,128)S(1)} %collective-permute-done.5, f32[1,3,7,128,128]{4,3,2,1,0:T(8,128)S(1)} %get-tuple-element.64, f32[3,8,128,128]{3,2,1,0:T(8,128)S(1)} %multiply_reduce_fusion, ...), kind=kLoop, calls=%fused_computation.71 | loop fusion | flops 10223615 | bytes 9441328 | tf_op jit(solution)/shard_map/reduce_sum | solution.py:90
  70.8 12.5 %all-reduce.15 = (f32[1]{0:T(128)}, f32[1]{0:T(128)}) all-reduce(f32[1]{0:T(128)} %bitcast.32, f32[1]{0:T(128)} %bitcast.37), channel_id=1, replica_groups=mesh['grp'=4,'slab'=8] {'slab'}, use_global_device_ids=true, to_apply=%region_8.9 | all-reduce | flops 2 | bytes 16 | tf_op jit(solution)/shard_map/psum | solution.py:94
  87.8 0.4 multiply_reduce_fusion.2
  88.2 4.3 %collective-permute-start.7 = (f32[1,3,1,128,128]{4,3,2,1,0:T(8,128)S(1)}, f32[1,3,1,128,128]{4,3,2,1,0:T(8,128)S(1)}, u32[]{:S(2)}, u32[]{:S(2)}) collective-permute-start(f32[1,3,1,128,128]{4,3,2,1,0:T(8,128)S(1)} %slice.203), channel_id=1, source_target_pairs={{1,0},{2,1},{3,2},{4,3},{5,4},{6,5},{7,6},{9,8},{10,9},{11,10},{12... | collective-permute-start | bytes 589832 | tf_op jit(solution)/shard_map/ppermute | solution.py:20
  92.5 2.1 collective-permute-start.6
  94.6 0.6 collective-permute-done.7
  95.2 1.8 collective-permute-done.6
  97.0 1.5 pad_maximum_fusion
  98.5 0.0 all-gather.2.cloned.1.call-update
  101.1 0.1 copy.12
  101.2 0.6 gather_fusion.1
  101.8 0.1 broadcast_select_fusion
  101.8 0.3 fusion.90
  102.2 0.1 reduce.17
  102.3 0.7 broadcast_select_fusion.1
  103.0 0.6 fusion.111
  103.6 1.9 fusion.96
  105.6 0.1 multiply_reduce_fusion.9
  105.7 0.1 fusion.93
  105.8 0.1 broadcast_multiply_fusion.2
  105.9 0.1 broadcast_multiply_fusion.1
  105.9 0.1 convert_add_fusion
  106.0 75.5 %all-gather.2.cloned.1.call-done = f32[4,3,10,128,128]{4,3,2,1,0:T(8,128)} async-done(((f32[1,3,10,128,128]{4,3,2,1,0:T(8,128)}), f32[4,3,10,128,128]{4,3,2,1,0:T(8,128)}) %all-gather.2.cloned.1.call-update) | async-done | bytes 7864336 | tf_op jit(solution)/shard_map/all_gather | solution.py:204
  181.5 19.9 %fusion.4 = f32[4,3,8,128,128]{4,2,3,1,0:T(8,128)S(1)} fusion(f32[4,3,10,128,128]{4,3,2,1,0:T(8,128)} %all-gather.2.cloned.1.call-done, f32[4]{0:T(128)S(1)} %fusion.96, f32[8]{0:T(128)S(1)} %compare_convert_fusion.5, f32[4,10]{1,0:T(4,128)S(1)} %convert_add_fusion, f32[4,8]{1,0:T(4,128)S(1)} %broadcast_multiply_fusion.2), kind=kOutput, calls=%fused_computation.12 | convolution fusion | flops 188745600 | bytes 14156112 | tf_op jit(solution)/shard_map/pkn,pcnyx->pckyx/dot_general | solution.py:134
  201.4 5.4 %fusion.2 = f32[3,8,128,128,1]{3,1,0,2,4:T(8,128)S(1)} fusion(f32[4,3,8,128,128]{4,2,3,1,0:T(8,128)S(1)} %fusion.4, f32[4,128]{1,0:T(4,128)S(1)} %fusion.93, f32[128]{0:T(128)S(1)} %compare_convert_fusion, f32[128]{0:T(128)S(1)} %convert_add_fusion.1, f32[4,128]{1,0:T(4,128)S(1)} %broadcast_multiply_fusion.1), kind=kOutput, calls=%fused_computation.4 | convolution fusion | flops 2416312320 | bytes 7869440 | tf_op jit(solution)/shard_map/pckyx,pmx->ckym/dot_general | solution.py:135
  206.8 0.1 copy.28
  206.9 1.4 copy.14
  (53 shorter events, 0.2 us)
Async XLA Ops:
  6.5 175.0 %all-gather.2.cloned.1.call-start = ((), (), s32[]{:S(2)}) async-start(), calls=%async_computation | async-start | bytes 9830400 | tf_op jit(solution)/shard_map/all_gather | solution.py:204
  12.3 6.9 %copy-start.17 = (f32[1,3,3]{2,0,1:T(1,128)S(1)}, f32[1,3,3]{2,0,1:T(1,128)}, u32[]{:S(2)}) copy-start(f32[1,3,3]{2,0,1:T(1,128)} %param.8) | copy-start | bytes 112
  12.3 7.0 %copy-start.18 = (f32[1,3,3]{2,0,1:T(1,128)S(1)}, f32[1,3,3]{2,0,1:T(1,128)}, u32[]{:S(2)}) copy-start(f32[1,3,3]{2,0,1:T(1,128)} %param.9) | copy-start | bytes 112
  12.5 7.6 %collective-permute-start.1 = (f32[1,1,1,128,128]{4,3,2,1,0:T(8,128)S(1)}, f32[1,1,1,128,128]{4,3,2,1,0:T(8,128)S(1)}, u32[]{:S(2)}, u32[]{:S(2)}) collective-permute-start(f32[1,1,1,128,128]{4,3,2,1,0:T(8,128)S(1)} %bitcast.95), channel_id=1, source_target_pairs={{0,1},{1,2},{2,3},{3,4},{4,5},{5,6},{6,7},{8,9},{9,10},{10,11},{11... | collective-permute-start | bytes 196616 | tf_op jit(solution)/shard_map/ppermute | solution.py:19
  17.1 5.6 %collective-permute-start = (f32[1,1,1,128,128]{4,3,2,1,0:T(8,128)S(1)}, f32[1,1,1,128,128]{4,3,2,1,0:T(8,128)S(1)}, u32[]{:S(2)}, u32[]{:S(2)}) collective-permute-start(f32[1,1,1,128,128]{4,3,2,1,0:T(8,128)S(1)} %slice.194), channel_id=1, source_target_pairs={{1,0},{2,1},{3,2},{4,3},{5,4},{6,5},{7,6},{9,8},{10,9},{11,10},{12... | collective-permute-start | bytes 196616 | tf_op jit(solution)/shard_map/ppermute | solution.py:20
  22.9 0.9 copy-start.15
  22.9 12.4 %copy-start.9 = (f32[8,128,128]{2,1,0:T(8,128)}, f32[8,128,128]{2,1,0:T(8,128)S(1)}, u32[]{:S(2)}) copy-start(f32[8,128,128]{2,1,0:T(8,128)S(1)} %get-tuple-element.61) | copy-start | bytes 1572868
  22.9 12.4 %copy-start.11 = (f32[8,128,128]{2,1,0:T(8,128)}, f32[8,128,128]{2,1,0:T(8,128)S(1)}, u32[]{:S(2)}) copy-start(f32[8,128,128]{2,1,0:T(8,128)S(1)} %get-tuple-element.63) | copy-start | bytes 1572868
  23.6 3.2 %copy-start.13 = (f32[8,128,128]{2,1,0:T(8,128)}, f32[8,128,128]{2,1,0:T(8,128)S(1)}, u32[]{:S(2)}) copy-start(f32[8,128,128]{2,1,0:T(8,128)S(1)} %get-tuple-element.74) | copy-start | bytes 1572868
  23.6 11.8 %copy-start.1 = (f32[8,128,128]{2,1,0:T(8,128)}, f32[8,128,128]{2,1,0:T(8,128)S(1)}, u32[]{:S(2)}) copy-start(f32[8,128,128]{2,1,0:T(8,128)S(1)} %get-tuple-element.72) | copy-start | bytes 1572868
  23.6 11.8 %copy-start.3 = (f32[8,128,128]{2,1,0:T(8,128)}, f32[8,128,128]{2,1,0:T(8,128)S(1)}, u32[]{:S(2)}) copy-start(f32[8,128,128]{2,1,0:T(8,128)S(1)} %get-tuple-element.73) | copy-start | bytes 1572868
  23.6 2.5 %copy-start = (f32[1,3,8,128,128]{4,3,2,1,0:T(8,128)S(1)}, f32[1,3,8,128,128]{4,3,2,1,0:T(8,128)}, u32[]{:S(2)}) copy-start(f32[1,3,8,128,128]{4,3,2,1,0:T(8,128)} %param.6) | copy-start | bytes 4718596
  23.8 3.0 %copy-start.14 = (f32[8,128,128]{2,1,0:T(8,128)}, f32[8,128,128]{2,1,0:T(8,128)S(1)}, u32[]{:S(2)}) copy-start(f32[8,128,128]{2,1,0:T(8,128)S(1)} %get-tuple-element.77) | copy-start | bytes 1572868
  23.8 11.6 %copy-start.5 = (f32[8,128,128]{2,1,0:T(8,128)}, f32[8,128,128]{2,1,0:T(8,128)S(1)}, u32[]{:S(2)}) copy-start(f32[8,128,128]{2,1,0:T(8,128)S(1)} %get-tuple-element.75) | copy-start | bytes 1572868
  23.8 11.6 %copy-start.7 = (f32[8,128,128]{2,1,0:T(8,128)}, f32[8,128,128]{2,1,0:T(8,128)S(1)}, u32[]{:S(2)}) copy-start(f32[8,128,128]{2,1,0:T(8,128)S(1)} %get-tuple-element.76) | copy-start | bytes 1572868
  27.2 7.0 %collective-permute-start.2 = (f32[1,3,1,128,128]{4,3,2,1,0:T(8,128)S(1)}, f32[1,3,1,128,128]{4,3,2,1,0:T(8,128)S(1)}, u32[]{:S(2)}, u32[]{:S(2)}) collective-permute-start(f32[1,3,1,128,128]{4,3,2,1,0:T(8,128)S(1)} %slice.197), channel_id=1, source_target_pairs={{1,0},{2,1},{3,2},{4,3},{5,4},{6,5},{7,6},{9,8},{10,9},{11,10},{12... | collective-permute-start | bytes 589832 | tf_op jit(solution)/shard_map/ppermute | solution.py:20
  29.1 6.2 %collective-permute-start.3 = (f32[1,3,1,128,128]{4,3,2,1,0:T(8,128)S(1)}, f32[1,3,1,128,128]{4,3,2,1,0:T(8,128)S(1)}, u32[]{:S(2)}, u32[]{:S(2)}) collective-permute-start(f32[1,3,1,128,128]{4,3,2,1,0:T(8,128)S(1)} %bitcast.91), channel_id=1, source_target_pairs={{0,1},{1,2},{2,3},{3,4},{4,5},{5,6},{6,7},{8,9},{9,10},{10,11},{11... | collective-permute-start | bytes 589832 | tf_op jit(solution)/shard_map/ppermute | solution.py:19
  59.8 7.0 %collective-permute-start.4 = (f32[1,3,1,128,128]{4,3,2,1,0:T(8,128)S(1)}, f32[1,3,1,128,128]{4,3,2,1,0:T(8,128)S(1)}, u32[]{:S(2)}, u32[]{:S(2)}) collective-permute-start(f32[1,3,1,128,128]{4,3,2,1,0:T(8,128)S(1)} %slice.200), channel_id=1, source_target_pairs={{1,0},{2,1},{3,2},{4,3},{5,4},{6,5},{7,6},{9,8},{10,9},{11,10},{12... | collective-permute-start | bytes 589832 | tf_op jit(solution)/shard_map/ppermute | solution.py:20
  61.9 6.1 %collective-permute-start.5 = (f32[1,3,1,128,128]{4,3,2,1,0:T(8,128)S(1)}, f32[1,3,1,128,128]{4,3,2,1,0:T(8,128)S(1)}, u32[]{:S(2)}, u32[]{:S(2)}) collective-permute-start(f32[1,3,1,128,128]{4,3,2,1,0:T(8,128)S(1)} %bitcast.89), channel_id=1, source_target_pairs={{0,1},{1,2},{2,3},{3,4},{4,5},{5,6},{6,7},{8,9},{9,10},{10,11},{11... | collective-permute-start | bytes 589832 | tf_op jit(solution)/shard_map/ppermute | solution.py:19
  65.4 2.6 %copy-start.2 = (f32[8,128,128]{2,1,0:T(8,128)S(1)}, f32[8,128,128]{2,1,0:T(8,128)}, u32[]{:S(2)}) copy-start(f32[8,128,128]{2,1,0:T(8,128)} %copy-done.1) | copy-start | bytes 1572868
  65.4 2.6 %copy-start.4 = (f32[8,128,128]{2,1,0:T(8,128)S(1)}, f32[8,128,128]{2,1,0:T(8,128)}, u32[]{:S(2)}) copy-start(f32[8,128,128]{2,1,0:T(8,128)} %copy-done.3) | copy-start | bytes 1572868
  65.4 2.6 %copy-start.6 = (f32[8,128,128]{2,1,0:T(8,128)S(1)}, f32[8,128,128]{2,1,0:T(8,128)}, u32[]{:S(2)}) copy-start(f32[8,128,128]{2,1,0:T(8,128)} %copy-done.5) | copy-start | bytes 1572868
  65.5 2.6 %copy-start.8 = (f32[8,128,128]{2,1,0:T(8,128)S(1)}, f32[8,128,128]{2,1,0:T(8,128)}, u32[]{:S(2)}) copy-start(f32[8,128,128]{2,1,0:T(8,128)} %copy-done.7) | copy-start | bytes 1572868
  65.5 2.6 %copy-start.10 = (f32[8,128,128]{2,1,0:T(8,128)S(1)}, f32[8,128,128]{2,1,0:T(8,128)}, u32[]{:S(2)}) copy-start(f32[8,128,128]{2,1,0:T(8,128)} %copy-done.9) | copy-start | bytes 1572868
  65.5 2.6 %copy-start.12 = (f32[8,128,128]{2,1,0:T(8,128)S(1)}, f32[8,128,128]{2,1,0:T(8,128)}, u32[]{:S(2)}) copy-start(f32[8,128,128]{2,1,0:T(8,128)} %copy-done.11) | copy-start | bytes 1572868
  88.2 7.0 %collective-permute-start.7 = (f32[1,3,1,128,128]{4,3,2,1,0:T(8,128)S(1)}, f32[1,3,1,128,128]{4,3,2,1,0:T(8,128)S(1)}, u32[]{:S(2)}, u32[]{:S(2)}) collective-permute-start(f32[1,3,1,128,128]{4,3,2,1,0:T(8,128)S(1)} %slice.203), channel_id=1, source_target_pairs={{1,0},{2,1},{3,2},{4,3},{5,4},{6,5},{7,6},{9,8},{10,9},{11,10},{12... | collective-permute-start | bytes 589832 | tf_op jit(solution)/shard_map/ppermute | solution.py:20
  92.5 4.5 %collective-permute-start.6 = (f32[1,3,1,128,128]{4,3,2,1,0:T(8,128)S(1)}, f32[1,3,1,128,128]{4,3,2,1,0:T(8,128)S(1)}, u32[]{:S(2)}, u32[]{:S(2)}) collective-permute-start(f32[1,3,1,128,128]{4,3,2,1,0:T(8,128)S(1)} %bitcast.90), channel_id=1, source_target_pairs={{0,1},{1,2},{2,3},{3,4},{4,5},{5,6},{6,7},{8,9},{9,10},{10,11},{11... | collective-permute-start | bytes 589832 | tf_op jit(solution)/shard_map/ppermute | solution.py:19
  98.5 2.6 %copy-start.16 = (s32[4,2]{0,1:T(2,128)S(1)}, s32[4,2]{0,1:T(2,128)}, u32[]{:S(2)}) copy-start(s32[4,2]{0,1:T(2,128)} %param.10) | copy-start | bytes 100
Sparse Core Ops, SparseCore 0:
  98.6 82.8 all-gather.1
where the time goes:
time: 217 us; the launch traced here: 215 us
  waiting for transfers between devices  84.8 us (39%)
  blocking collectives  27.6 us (13%)
  matrix products  25.2 us (12%)
  between operations  25 us (12%)
  starting transfers between devices  24 us (11%)
  other arithmetic  21 us (10%)
  local copies, waits for them, and re-layouts  7.54 us (3%)
    all_gather x1, waiting for transfers between devices, per_device(): pieces = lax.all_gather(extended, 'grp', axis=0, tiled=True)  75.5 us
    psum x2, blocking collectives, joint_totals(): lax.psum((pair_sums(residual, precond), pair_sums(precond, applied)), 'sl...  27.6 us
    dot_general x1, matrix products, contribute(): jnp.einsum('pkn,pcnyx->pckyx', weight_z, pieces, precision=exact_mode)  19.9 us
    ppermute x4, starting transfers between devices, padded_2(): before = lax.ppermute(last, axis, up)  13.8 us
    ppermute x4, starting transfers between devices, padded_2(): after = lax.ppermute(leading, axis, down)  10.2 us
    reduce_sum x2, other arithmetic, pair_sums(): return jnp.sum(first * second, axis=(1, 2, 3, 4))  6.65 us
    dot_general x1, matrix products, contribute(): jnp.einsum('pckyx,pmx->ckym', vertical, weight_x, precision=exact_mode)  5.36 us
    ppermute x4, waiting for transfers between devices, padded_2(): after = lax.ppermute(leading, axis, down)  5.07 us
  transfers between devices with their start and end apart: 9, of which 8 were waited for; matrix products, arithmetic and copies ran while one was open for 3% of the time, Pallas kernels for 0%

commit v1 on v0

v1 whole, which is shorter than its diff:
```python
import functools

import jax
import jax.numpy as jnp
from jax import lax
from jax.experimental import pallas as pl
from jax.experimental.pallas import tpu as pltpu
from jax.sharding import PartitionSpec as P

CHUNK = 32
PAD = 8
VMEM_SPEC = pl.BlockSpec(memory_space=pltpu.VMEM)
SMEM_SPEC = pl.BlockSpec(memory_space=pltpu.SMEM)
ANY_SPEC = pl.BlockSpec(memory_space=pl.ANY)
f32 = jnp.float32


def shape_of(*dims):
    return jax.ShapeDtypeStruct(dims, f32)


def estimate(flops, nbytes):
    return pl.CostEstimate(flops=int(flops), bytes_accessed=int(nbytes), transcendentals=0)


def cells(full, level):
    return lax.shift_right_logical(jnp.int32(full), 2 - level)


def lanes(rows, width):
    return lax.broadcasted_iota(jnp.int32, (rows, width), 1)


def coefficients(an, nx, nz, height):
    wx = nx.astype(f32) / height
    wz = nz.astype(f32) / height
    wx, wz = wx * wx, wz * wz
    return [[an[c, 0] * wx, an[c, 1], an[c, 2] * wz] for c in range(3)]


def fold(values):
    rows = values.shape[0]
    total = values[0:8]
    for start in range(8, rows, 8):
        total = total + values[start : start + 8]
    return total


def rims_kernel(lev, f_hbm, k_hbm, up, dn, sems):
    depth = f_hbm.shape[1]
    a = cells(depth, lev[lax.axis_index("grp"), 1])
    copies = [
        (f_hbm.at[:, a - 1], up.at[0:3]),
        (k_hbm.at[:, a - 1], up.at[3:6]),
        (k_hbm.at[2, a - 2], up.at[6]),
        (f_hbm.at[:, 0], dn.at[0:3]),
        (k_hbm.at[:, 0], dn.at[3:6]),
        (k_hbm.at[2, 1], dn.at[6]),
    ]
    started = [pltpu.make_async_copy(s, d, sems.at[i]) for i, (s, d) in enumerate(copies)]
    for copy in started:
        copy.start()
    for copy in started:
        copy.wait()


def first_kernel(slabs, lev, an, cp, f, k, lo, hi, zs, w, wl, gx, gys, gz, gl, dots, rj, kys, kzs):
    _, depth, height, width = f.shape
    g = lax.axis_index("grp")
    nx = cells(width, lev[g, 0])
    a = cells(depth, lev[g, 1])
    co = coefficients(an, nx, a * slabs, height)
    lane = lanes(CHUNK, width)
    in_x = lane < nx
    in_xp = lane < nx - 1
    in_xm = lane > 0
    chunks = range(0, height, CHUNK)
    zero_pad = jnp.zeros((PAD, width), f32)

    def keep(values):
        return jnp.where(in_x, values, 0.0)

    def pad_row(row):
        kys[row, 0:PAD] = zero_pad
        kys[row, height + PAD :] = zero_pad
        for c in range(3):
            zs[c, row, 0:PAD] = zero_pad
            zs[c, row, height + PAD :] = zero_pad

    def stage(row, _):
        pad_row(row + 1)
        for y in chunks:
            kys[row + 1, PAD + y : PAD + y + CHUNK] = keep(k[1, row, y : y + CHUNK])
            kzs[row + 2, y : y + CHUNK] = keep(k[2, row, y : y + CHUNK])
        return 0

    lax.fori_loop(0, a, stage, 0)
    pad_row(0)
    pad_row(a + 1)
    for y in chunks:
        here = slice(y, y + CHUNK)
        kys[0, PAD + y : PAD + y + CHUNK] = keep(lo[4, here])
        kys[a + 1, PAD + y : PAD + y + CHUNK] = keep(hi[4, here])
        kzs[0, here] = keep(lo[6, here])
        kzs[1, here] = keep(lo[5, here])
        kzs[a + 2, here] = keep(hi[5, here])
        kzs[a + 3, here] = keep(hi[6, here])

    def jacobi(f_at, kx_at, row, own):
        for y in chunks:
            kx = keep(kx_at(y))
            kxp = jnp.where(in_xp, pltpu.roll(kx, width - 1, 1), 0.0)
            kxm = jnp.where(in_xm, pltpu.roll(kx, 1, 1), 0.0)
            ky = kys[row, PAD + y : PAD + y + CHUNK]
            kyp = kys[row, PAD + y + 1 : PAD + y + 1 + CHUNK]
            kym = kys[row, PAD + y - 1 : PAD + y - 1 + CHUNK]
            kz = kzs[row + 1, y : y + CHUNK]
            kzp = kzs[row + 2, y : y + CHUNK]
            kzm = kzs[row, y : y + CHUNK]
            sx = kx + 0.5 * (kxp + kxm)
            sy = ky + 0.5 * (kyp + kym)
            sz = kz + 0.5 * (kzp + kzm)
            for c in range(3):
                diagonal = cp[c, c] + co[c][0] * sx + co[c][1] * sy + co[c][2] * sz
                inverse = 1.0 / diagonal
                zs[c, row, PAD + y : PAD + y + CHUNK] = keep(f_at(c, y)) * inverse
                if own:
                    rj[c, row - 1, y : y + CHUNK] = inverse
            if own:
                gx[row - 1, y : y + CHUNK] = jnp.where(in_xp, 0.5 * (kx + kxp), 0.0)
                gys[row - 1, PAD + y : PAD + y + CHUNK] = 0.5 * (ky + kyp)
                gz[row - 1, y : y + CHUNK] = 0.5 * (kz + kzp)

    def own_row(row, _):
        gys[row, 0:PAD] = zero_pad
        jacobi(
            lambda c, y: f[c, row, y : y + CHUNK], lambda y: k[0, row, y : y + CHUNK], row + 1, True
        )
        return 0

    jacobi(lambda c, y: lo[c, y : y + CHUNK], lambda y: lo[3, y : y + CHUNK], 0, False)
    jacobi(lambda c, y: hi[c, y : y + CHUNK], lambda y: hi[3, y : y + CHUNK], a + 1, False)
    lax.fori_loop(0, a, own_row, 0)
    for y in chunks:
        gl[y : y + CHUNK] = 0.5 * (kzs[1, y : y + CHUNK] + kzs[2, y : y + CHUNK])

    def image_row(row, sums):
        s0, s1, s2 = sums
        for c in range(3):
            w[c, row, height:] = zero_pad
        for y in chunks:
            here = slice(y, y + CHUNK)
            mid = slice(PAD + y, PAD + y + CHUNK)
            above = slice(PAD + y + 1, PAD + y + 1 + CHUNK)
            below = slice(PAD + y - 1, PAD + y - 1 + CHUNK)
            fx = gx[row, here]
            fyp, fym = gys[row, mid], gys[row, below]
            fzp = gz[row, here]
            fzm = 0.5 * (kzs[row + 1, here] + kzs[row + 2, here])
            z = [zs[c, row + 1, mid] for c in range(3)]
            for c in range(3):
                tx = fx * pltpu.roll(z[c], width - 1, 1) + pltpu.roll(fx * z[c], 1, 1)
                ty = fyp * zs[c, row + 1, above] + fym * zs[c, row + 1, below]
                tz = fzp * zs[c, row + 2, mid] + fzm * zs[c, row, mid]
                v = co[c][0] * tx + co[c][1] * ty + co[c][2] * tz
                for other in range(3):
                    if other != c:
                        v = v - cp[c, other] * z[other]
                force = keep(f[c, row, here])
                image = force - v
                scaled = z[c] - v * rj[c, row, here]
                w[c, row, here] = scaled
                s0 = s0 + fold(force * z[c])
                s1 = s1 + fold(image * z[c])
                s2 = s2 + fold(image * scaled)
        return s0, s1, s2

    nothing = jnp.zeros((8, width), f32)
    s0, s1, s2 = lax.fori_loop(0, a, image_row, (nothing, nothing, nothing))
    for c in range(3):
        for y in chunks:
            wl[c, y : y + CHUNK] = w[c, a - 1, y : y + CHUNK]
    dots[...] = jnp.zeros((8, width), f32)
    for i, total in enumerate((s0, s1, s2)):
        dots[i : i + 1, :] = jnp.sum(total, axis=0, keepdims=True)


def second_kernel(slabs, lev, an, cp, w, gx, gys, gz, part):
    depth, height, width = gx.shape
    g = lax.axis_index("grp")
    nx = cells(width, lev[g, 0])
    a = cells(depth, lev[g, 1])
    co = coefficients(an, nx, a * slabs, height)

    def row_sum(row, total, inner):
        for y in range(0, height, CHUNK):
            here = slice(y, y + CHUNK)
            fx, fy = gx[row, here], gys[row, PAD + y : PAD + y + CHUNK]
            fz = gz[row, here] if inner else None
            own = [w[c, row, here] for c in range(3)]
            for c in range(3):
                v = co[c][0] * (fx * pltpu.roll(own[c], width - 1, 1))
                v = v + co[c][1] * (fy * w[c, row, y + 1 : y + 1 + CHUNK])
                if inner:
                    v = v + co[c][2] * (fz * w[c, row + 1, here])
                if c < 2:
                    v = v - cp[c, c + 1] * own[c + 1]
                if c == 0:
                    v = v - cp[0, 2] * own[2]
                total = total + fold(v * own[c])
        return total

    total = lax.fori_loop(
        0, a - 1, lambda row, t: row_sum(row, t, True), jnp.zeros((8, width), f32)
    )
    part[...] = 2.0 * row_sum(a - 1, total, False)


def cross_kernel(slabs, lev, an, w, gl, wlo, part, dots, out):
    depth, height, width = w.shape[1], gl.shape[0], gl.shape[1]
    g = lax.axis_index("grp")
    nx = cells(width, lev[g, 0])
    a = cells(depth, lev[g, 1])
    co = coefficients(an, nx, a * slabs, height)
    total = jnp.zeros((8, width), f32)
    for y in range(0, height, CHUNK):
        here = slice(y, y + CHUNK)
        v = jnp.zeros((CHUNK, width), f32)
        for c in range(3):
            v = v + co[c][2] * (w[c, 0, here] * wlo[c, here])
        total = total + fold(gl[here] * v)
    out[...] = dots[...]
    out[3:4, :] = jnp.sum(part[...] + 2.0 * total, axis=0, keepdims=True)


def solution_kernel(lev, mine, theirs, zs, w, u, h1, h2):
    _, depth, height, width = u.shape
    half = depth // 2
    quarter = half // 2
    g = lax.axis_index("grp")
    a = cells(depth, lev[g, 1])
    narrow = lev[g, 0] < 2
    sums = jnp.sum(mine[...] + theirs[...], axis=1, keepdims=True)
    sums = jnp.broadcast_to(sums, (8, width))
    d0, d1, d2, e3 = sums[0:1], sums[1:2], sums[2:3], sums[3:4]
    d3 = d2 - e3
    first = d0 / d1
    rz = first * first * d2 - d0
    more = 1.0 + rz / d0
    bend = more * more * d1 - 2.0 * first * more * d2 + first * first * d3
    second = rz / bend
    alpha = jnp.broadcast_to(first + second * more, (CHUNK, width))
    beta = jnp.broadcast_to(-second * first, (CHUNK, width))
    chunks = range(0, height, CHUNK)

    def active_row(row, _):
        for c in range(3):
            for y in chunks:
                z = zs[c, row + 1, PAD + y : PAD + y + CHUNK]
                u[c, row, y : y + CHUNK] = alpha * z + beta * w[c, row, y : y + CHUNK]
        return 0

    def idle_row(row, _):
        for c in range(3):
            for y in chunks:
                u[c, row, y : y + CHUNK] = jnp.zeros((CHUNK, width), f32)
        return 0

    lax.fori_loop(0, a, active_row, 0)
    lax.fori_loop(a, depth, idle_row, 0)
    share = jnp.where(narrow, 1.0, 0.0)
    for n in range(half):
        target, slot = (h1, n) if n < quarter else (h2, n - quarter)
        for c in range(3):
            for y in chunks:
                here = slice(y, y + CHUNK)
                beside = pltpu.roll(u[c, n + half, here], width // 2, 1)
                target[c, slot, here] = u[c, n, here] + share * beside


def role(lev, nb, g, p):
    n0, n1, n2 = nb[g, 0], nb[g, 1], nb[g, 2]
    sign = jnp.where(n2 == p, 1.0, 0.0) - jnp.where((n0 == p) | (n1 == p), 1.0, 0.0)
    coarse = lev[p, 1] < lev[g, 1]
    return sign.astype(f32), coarse


def x_weights(lev, g, p, sign, width):
    to_x = cells(width, lev[g, 0])
    from_x = cells(width, lev[p, 0])
    source = lax.broadcasted_iota(jnp.int32, (width, 2 * width), 0)
    target = lax.broadcasted_iota(jnp.int32, (width, 2 * width), 1)
    second = target >= width
    target = jnp.where(second, target - width, target)
    shift = jnp.where(second, width // 2, 0)
    cell = source - shift
    ratio = from_x.astype(f32) / to_x.astype(f32)
    along = (target.astype(f32) + 0.5) * ratio
    weight = jnp.maximum(0.0, 1.0 - jnp.abs(along - (cell.astype(f32) + 0.5)))
    fits = (target < to_x) & (cell >= 0) & (cell < from_x)
    fits = fits & (jnp.logical_not(second) | (lev[p, 0] < 2))
    return jnp.where(fits, weight * sign, 0.0).astype(jnp.bfloat16)


def split_dot(values, weights):
    high = values.astype(jnp.bfloat16)
    rest = values - high.astype(f32)
    middle = rest.astype(jnp.bfloat16)
    low = (rest - middle.astype(f32)).astype(jnp.bfloat16)
    dot = functools.partial(jnp.dot, preferred_element_type=f32)
    return dot(high, weights) + (dot(middle, weights) + dot(low, weights))


def edges_kernel(others, lev, nb, *refs):
    pieces = refs[: 2 * len(others)]
    up, dn, weights = refs[2 * len(others) :]
    _, quarter, height, width = pieces[0].shape
    depth = 4 * quarter
    g = lax.axis_index("grp")
    up[...] = jnp.zeros(up.shape, f32)
    dn[...] = jnp.zeros(dn.shape, f32)
    for i, other in enumerate(others):
        h1, h2 = pieces[2 * i], pieces[2 * i + 1]
        p = other(g)
        sign, coarse = role(lev, nb, g, p)

        @pl.when((sign != 0.0) & coarse)
        def _():
            weights[...] = x_weights(lev, g, p, sign, width)[:, :width]
            last = cells(depth, lev[p, 1]) - 1
            in_first = last < quarter
            i1 = jnp.minimum(last, quarter - 1)
            i2 = jnp.maximum(last - quarter, 0)
            for c in range(3):
                dn[c] += 0.25 * split_dot(h1[c, 0], weights[...])
                row = jnp.where(in_first, h1[c, i1], h2[c, i2])
                up[c] += 0.25 * split_dot(row, weights[...])


def mix_kernel(others, lev, nb, u, *refs):
    pieces = refs[: 2 * len(others)]
    out, weights = refs[2 * len(others) :]
    _, depth, height, width = u.shape
    half = depth // 2
    quarter = half // 2
    g = lax.axis_index("grp")
    run = cells(depth, lev[g, 1])
    for c in range(3):
        for row in range(depth):
            out[c, row] = u[c, row]
    for i, other in enumerate(others):
        p = other(g)
        sign, coarse = role(lev, nb, g, p)

        def plane(c, n):
            ref, slot = (pieces[2 * i], n) if n < quarter else (pieces[2 * i + 1], n - quarter)
            return ref[c, slot]

        @pl.when(sign != 0.0)
        def _():
            weights[...] = x_weights(lev, g, p, sign, width)

        @pl.when((sign != 0.0) & jnp.logical_not(coarse))
        def _():
            def component(c, _):
                for n in range(half):
                    both = split_dot(plane(c, n), weights[...])
                    out[c, n] += both[:, :width]
                    out[c, n + half] += both[:, width:]
                return 0

            lax.fori_loop(0, 3, component, 0)

        @pl.when((sign != 0.0) & coarse)
        def _():
            def component(c, _):
                for n in range(half):
                    one = split_dot(plane(c, n), weights[:, :width])
                    out[c, 2 * n] += 0.75 * one
                    out[c, 2 * n + 1] += 0.75 * one
                    if n > 0:
                        out[c, 2 * n - 1] += 0.25 * one
                    if n < half - 1:
                        share = jnp.where(2 * n + 2 < run, 0.25, 0.0)
                        out[c, 2 * n + 2] += share * one
                return 0

            lax.fori_loop(0, 3, component, 0)


def finish_kernel(lev, lo, hi, given, out, first, last, sems):
    depth = out.shape[1]
    run = cells(depth, lev[lax.axis_index("grp"), 1])
    reads = [
        pltpu.make_async_copy(given.at[:, 0], first, sems.at[0]),
        pltpu.make_async_copy(given.at[:, run - 1], last, sems.at[1]),
    ]
    for copy in reads:
        copy.start()
    for copy in reads:
        copy.wait()
    first[...] += lo[...]
    last[...] += hi[...]
    writes = [
        pltpu.make_async_copy(first, out.at[:, 0], sems.at[0]),
        pltpu.make_async_copy(last, out.at[:, run - 1], sems.at[1]),
    ]
    for copy in writes:
        copy.start()
    for copy in writes:
        copy.wait()


def permute_up(values):
    slabs = lax.axis_size("slab")
    return lax.ppermute(values, "slab", [(i, i + 1) for i in range(slabs - 1)])


def permute_down(values):
    slabs = lax.axis_size("slab")
    return lax.ppermute(values, "slab", [(i + 1, i) for i in range(slabs - 1)])


def along(values, axis, step):
    peers = lax.axis_size(axis)
    return lax.ppermute(values, axis, [(i, i ^ step) for i in range(peers)])


def slab_sums(sums):
    slabs = lax.axis_size("slab")
    step = 1
    while 2 * step < slabs:
        sums = sums + along(sums, "slab", step)
        step *= 2
    return sums, along(sums, "slab", step)


def gather(h1, h2):
    groups = lax.axis_size("grp")
    if groups == 4:
        a1, b2 = along(h1, "grp", 1), along(h2, "grp", 2)
        a2, b1 = along(h2, "grp", 1), along(h1, "grp", 2)
        c1, c2 = along(a1, "grp", 2), along(b2, "grp", 1)
        return [(1, a1, a2), (2, b1, b2), (3, c1, c2)]
    return [(step, along(h1, "grp", step), along(h2, "grp", step)) for step in range(1, groups)]


def call(kernel, outs, specs_in, specs_out, scratch=(), cost=None, **more):
    return pl.pallas_call(
        kernel,
        out_shape=outs,
        in_specs=specs_in,
        out_specs=specs_out,
        scratch_shapes=list(scratch),
        cost_estimate=cost,
        **more,
    )


def per_device(forcing, stiffness, anisotropy, coupling, levels, neighbours):
    _, _, depth, height, width = forcing.shape
    slabs = lax.axis_size("slab")
    quarter = depth // 4
    f, k = forcing[0], stiffness[0]
    an, cp = anisotropy[0], coupling[0]
    plane = 4 * height * width
    padded = height + 2 * PAD
    dma = pltpu.SemaphoreType.DMA

    up, dn = call(
        rims_kernel,
        [shape_of(7, height, width)] * 2,
        [SMEM_SPEC, ANY_SPEC, ANY_SPEC],
        [VMEM_SPEC] * 2,
        [dma((6,))],
        estimate(0, 28 * plane),
        name="rims",
    )(levels, f, k)
    lo, hi = permute_up(up), permute_down(dn)

    zs, w, wl, gx, gys, gz, gl, dots = call(
        functools.partial(first_kernel, slabs),
        [
            shape_of(3, depth + 2, padded, width),
            shape_of(3, depth, height + PAD, width),
            shape_of(3, height, width),
            shape_of(depth, height, width),
            shape_of(depth, height + PAD, width),
            shape_of(depth, height, width),
            shape_of(height, width),
            shape_of(8, width),
        ],
        [SMEM_SPEC] * 3 + [VMEM_SPEC] * 4,
        [VMEM_SPEC] * 8,
        [
            pltpu.VMEM((3, depth, height, width), f32),
            pltpu.VMEM((depth + 2, padded, width), f32),
            pltpu.VMEM((depth + 4, height, width), f32),
        ],
        estimate(150 * depth * plane, 150 * plane),
        name="first",
    )(levels, an, cp, f, k, lo, hi)
    wlo = permute_up(wl)
    part = call(
        functools.partial(second_kernel, slabs),
        shape_of(8, width),
        [SMEM_SPEC] * 3 + [VMEM_SPEC] * 4,
        VMEM_SPEC,
        cost=estimate(30 * depth * plane, 50 * plane),
        name="second",
    )(levels, an, cp, w, gx, gys, gz)
    dots = call(
        functools.partial(cross_kernel, slabs),
        shape_of(8, width),
        [SMEM_SPEC] * 2 + [VMEM_SPEC] * 5,
        VMEM_SPEC,
        cost=estimate(8 * plane, 6 * plane),
        name="cross",
    )(levels, an, w, gl, wlo, part, dots)
    mine, theirs = slab_sums(dots)
    u, h1, h2 = call(
        solution_kernel,
        [shape_of(3, depth, height, width)] + [shape_of(3, quarter, height, width)] * 2,
        [SMEM_SPEC] + [VMEM_SPEC] * 4,
        [VMEM_SPEC] * 3,
        cost=estimate(4 * depth * plane, 90 * plane),
        name="solve",
    )(levels, mine, theirs, zs, w)
    received = gather(h1, h2)
    others = [functools.partial(lambda step, g: g ^ step, step) for step, _, _ in received]
    pieces = [piece for _, first, second in received for piece in (first, second)]
    edge_up, edge_dn = call(
        functools.partial(edges_kernel, others),
        [shape_of(3, height, width)] * 2,
        [SMEM_SPEC] * 2 + [VMEM_SPEC] * len(pieces),
        [VMEM_SPEC] * 2,
        [pltpu.VMEM((width, width), jnp.bfloat16)],
        estimate(100 * plane, 40 * plane),
        name="edges",
    )(levels, neighbours, *pieces)
    from_lo, from_hi = permute_up(edge_up), permute_down(edge_dn)
    mixed = call(
        functools.partial(mix_kernel, others),
        shape_of(3, depth, height, width),
        [SMEM_SPEC] * 2 + [VMEM_SPEC] * (1 + len(pieces)),
        VMEM_SPEC,
        [pltpu.VMEM((width, 2 * width), jnp.bfloat16)],
        estimate(2000 * plane, 90 * plane),
        name="mix",
    )(levels, neighbours, u, *pieces)
    mixed = call(
        finish_kernel,
        shape_of(3, depth, height, width),
        [SMEM_SPEC] + [VMEM_SPEC] * 2 + [ANY_SPEC],
        ANY_SPEC,
        [
            pltpu.VMEM((3, height, width), f32),
            pltpu.VMEM((3, height, width), f32),
            dma((2,)),
        ],
        estimate(0, 18 * plane),
        input_output_aliases={3: 0},
        name="finish",
    )(levels, from_lo, from_hi, mixed)
    return mixed[None]


def solution(mesh):
    return jax.shard_map(
        per_device,
        mesh=mesh,
        in_specs=(
            P("grp", None, "slab", None, None),
            P("grp", None, "slab", None, None),
            P("grp", None, None),
            P("grp", None, None),
            P(),
            P(),
        ),
        out_specs=P("grp", None, "slab", None, None),
        check_vma=False,
    )
```

time: 217 us -> 96.5 us (0.44)
  waiting for transfers between devices: 84.8 us -> 33.3 us
  Pallas kernels: 0 us -> 29.4 us
  blocking collectives: 27.6 us -> 0 us
  matrix products: 25.2 us -> 0 us
  between operations: 25 us -> 0.12 us
  other arithmetic: 21 us -> 0.67 us
  starting transfers between devices: 24 us -> 26.4 us
    all_gather x1 -> x0, waiting for transfers between devices: 75.5 us -> none  [per_device(): pieces = lax.all_gather(extended, 'grp', axis=0, tiled=True)]
    pallas_call x0 -> x8, Pallas kernels: none -> 29.4 us  [the longest x1 8.15 us: per_device(): call(functools.partial(first_kernel, slabs), [shape_of(3, depth + 2, padd...]
    psum x2 -> x0, blocking collectives: 27.6 us -> none  [joint_totals(): lax.psum((pair_sums(residual, precond), pair_sums(precond, applied)), 'sl...]
    dot_general x2 -> x0, matrix products: 25.2 us -> none  [the longest x1 19.9 us: contribute(): jnp.einsum('pkn,pcnyx->pckyx', weight_z, pieces, precision=exact_mode)]
    ppermute x8 -> x14, waiting for transfers between devices: 9.24 us -> 33.3 us  [the longest x9 23.9 us: along(): return lax.ppermute(values, axis, [(i, i ^ step) for i in range(peers)])]
    reduce_sum x8 -> x0, other arithmetic: 12.4 us -> none  [the longest x2 6.65 us: pair_sums(): return jnp.sum(first * second, axis=(1, 2, 3, 4))]
    unnamed x40 -> x32, local copies, waits for them, and re-layouts: 2.48 us -> 6.14 us
    mul x9 -> x0, other arithmetic: 2.91 us -> none  [the longest x1 1.52 us: per_device(): kept = stiffness * active]
  transfers between devices with their start and end apart: 9 -> 14, of which waited for: 8 -> 9; matrix products, arithmetic and copies ran while one was open for 3% -> 1% of each run, Pallas kernels for 0% -> 7%
where the time goes in v1:
time: 96.5 us; the launch traced here: 96 us
  waiting for transfers between devices  33.3 us (35%)
  Pallas kernels  29.4 us (30%)
  starting transfers between devices  26.4 us (27%)
  local copies, waits for them, and re-layouts  6.14 us (6%)
    ppermute x9, waiting for transfers between devices, along(): return lax.ppermute(values, axis, [(i, i ^ step) for i in range(peers)])  23.9 us
    ppermute x3, starting transfers between devices, permute_up(): return lax.ppermute(values, 'slab', [(i, i + 1) for i in range(slabs - 1)])  13.1 us
    ppermute x9, starting transfers between devices, along(): return lax.ppermute(values, axis, [(i, i ^ step) for i in range(peers)])  9.51 us
    pallas_call x1, Pallas kernels, per_device(): call(functools.partial(first_kernel, slabs), [shape_of(3, depth + 2, padd...  8.15 us
    ppermute x2, waiting for transfers between devices, permute_down(): return lax.ppermute(values, 'slab', [(i + 1, i) for i in range(slabs - 1)])  6.17 us
    unnamed x32, local copies, waits for them, and re-layouts  6.14 us
    pallas_call x1, Pallas kernels, per_device(): call(solution_kernel, [shape_of(3, depth, height, width)] + [shape_of(3,...  3.87 us
    ppermute x2, starting transfers between devices, permute_down(): return lax.ppermute(values, 'slab', [(i + 1, i) for i in range(slabs - 1)])  3.84 us
  transfers between devices with their start and end apart: 14, of which 9 were waited for; matrix products, arithmetic and copies ran while one was open for 1% of the time, Pallas kernels for 7%

profile of v1, /device:TPU:1, one launch (start us, length us, event | category | flops | bytes accessed | tf_op | source)
XLA Modules:
  0.0 96.0 jit_solution(9080297795134397731)
XLA Ops:
  0.0 1.3 %copy.15.lev = s32[4,2]{1,0:T(4,128)} copy(s32[4,2]{0,1:T(2,128)} %param.10) | data formatting | bytes 64 | tf_op args[4]
  1.3 0.0 copy-start.13
  1.4 0.0 copy-start.14
  1.4 3.1 %rims.1 = (f32[7,128,128]{2,1,0:T(8,128)}, f32[7,128,128]{2,1,0:T(8,128)}) custom-call(s32[4,2]{1,0:T(4,128)} %copy.15.lev, f32[3,8,128,128]{3,2,1,0:T(8,128)} %bitcast.7, f32[3,8,128,128]{3,2,1,0:T(8,128)} %bitcast.9), custom_call_target="tpu_custom_call" | custom-call | bytes 1835008 | tf_op jit(solution)/shard_map/rims/pallas_call | solution.py:470
  4.4 4.6 %collective-permute-start = (f32[7,128,128]{2,1,0:T(8,128)}, f32[7,128,128]{2,1,0:T(8,128)S(1)}, u32[]{:S(2)}, u32[]{:S(2)}) collective-permute-start(f32[7,128,128]{2,1,0:T(8,128)} %get-tuple-element.20), channel_id=1, source_target_pairs={{0,1},{1,2},{2,3},{3,4},{4,5},{5,6},{6,7},{8,9},{9,10},{10,11},{11... | collective-permute-start | bytes 1376264 | tf_op jit(solution)/shard_map/ppermute | solution.py:416
  9.0 1.9 %collective-permute-start.1 = (f32[7,128,128]{2,1,0:T(8,128)}, f32[7,128,128]{2,1,0:T(8,128)S(1)}, u32[]{:S(2)}, u32[]{:S(2)}) collective-permute-start(f32[7,128,128]{2,1,0:T(8,128)} %get-tuple-element.21), channel_id=1, source_target_pairs={{1,0},{2,1},{3,2},{4,3},{5,4},{6,5},{7,6},{9,8},{10,9},{11,10},{12... | collective-permute-start | bytes 1376264 | tf_op jit(solution)/shard_map/ppermute | solution.py:421
  10.9 0.0 copy-done.13
  10.9 0.0 copy-done.14
  11.0 0.6 copy_bitcast_fusion
  11.5 3.2 %collective-permute-done.lo = f32[7,128,128]{2,1,0:T(8,128)S(1)} collective-permute-done((f32[7,128,128]{2,1,0:T(8,128)}, f32[7,128,128]{2,1,0:T(8,128)S(1)}, u32[]{:S(2)}, u32[]{:S(2)}) %collective-permute-start) | collective-permute-done | bytes 458784 | tf_op jit(solution)/shard_map/ppermute | solution.py:416
  14.7 0.0 copy-start.6
  14.7 4.3 %collective-permute-done.1.hi = f32[7,128,128]{2,1,0:T(8,128)S(1)} collective-permute-done((f32[7,128,128]{2,1,0:T(8,128)}, f32[7,128,128]{2,1,0:T(8,128)S(1)}, u32[]{:S(2)}, u32[]{:S(2)}) %collective-permute-start.1) | collective-permute-done | bytes 458784 | tf_op jit(solution)/shard_map/ppermute | solution.py:421
  19.0 0.0 copy-start.7
  19.0 0.0 copy-done.6
  19.0 0.8 copy-done.7
  19.8 8.2 %first.1 = (f32[3,10,144,128]{3,2,1,0:T(8,128)}, f32[3,8,136,128]{3,2,1,0:T(8,128)}, f32[3,128,128]{2,1,0:T(8,128)}, f32[8,128,128]{2,1,0:T(8,128)}, f32[8,136,1...) custom-call(s32[4,2]{1,0:T(4,128)} %copy.15.lev, f32[3,3]{1,0:T(4,128)} %get-tuple-element.36.an, ...), custom_call_target="tpu_custom_call" | custom-call | flops 78643200 | bytes 9830400 | tf_op jit(solution)/shard_map/first/pallas_call | solution.py:481
  27.9 1.9 %collective-permute-start.2 = (f32[3,128,128]{2,1,0:T(8,128)}, f32[3,128,128]{2,1,0:T(8,128)S(1)}, u32[]{:S(2)}, u32[]{:S(2)}) collective-permute-start(f32[3,128,128]{2,1,0:T(8,128)} %get-tuple-element.24), channel_id=1, source_target_pairs={{0,1},{1,2},{2,3},{3,4},{4,5},{5,6},{6,7},{8,9},{9,10},{10,11},{11... | collective-permute-start | bytes 589832 | tf_op jit(solution)/shard_map/ppermute | solution.py:416
  29.9 3.6 %second.1.part = f32[8,128]{1,0:T(8,128)} custom-call(s32[4,2]{1,0:T(4,128)} %copy.15.lev, f32[3,3]{1,0:T(4,128)} %get-tuple-element.36.an, f32[3,3]{1,0:T(4,128)} %get-tuple-element.35.cp, f32[3,8,136,128]{3,2,1,0:T(8,128)} %get-tuple-element.22.w, f32[8,128,128]{2,1,0:T(8,128)} %get-tuple-element.25.gx, f32[8,136,128]{2,1,0:T(8,128)} %get-tuple-element.26.gys, ...), custom_call_target="tpu_custom_call" | custom-call | flops 15728640 | bytes 3276800 | tf_op jit(solution)/shard_map/second/pallas_call | solution.py:504
  33.4 0.0 collective-permute-done.2.wlo
  33.4 0.0 copy-start.10
  33.4 0.7 copy-done.10
  34.1 2.1 %cross.1 = f32[8,128]{1,0:T(8,128)} custom-call(s32[4,2]{1,0:T(4,128)} %copy.15.lev, f32[3,3]{1,0:T(4,128)} %get-tuple-element.36.an, f32[3,8,136,128]{3,2,1,0:T(8,128)} %get-tuple-element.22.w, f32[128,128]{1,0:T(8,128)} %get-tuple-element.23.gl, f32[3,128,128]{2,1,0:T(8,128)} %copy-done.10, f32[8,128]{1,0:T(8,128)} %second.1.part, ...), custom_call_target="tpu_custom_call" | custom-call | flops 524288 | bytes 393216 | tf_op jit(solution)/shard_map/cross/pallas_call | solution.py:512
  36.2 0.5 collective-permute-start.3
  36.8 1.0 %collective-permute-done.3 = f32[8,128]{1,0:T(8,128)S(1)} collective-permute-done((f32[8,128]{1,0:T(8,128)}, f32[8,128]{1,0:T(8,128)S(1)}, u32[]{:S(2)}, u32[]{:S(2)}) %collective-permute-start.3) | collective-permute-done | bytes 4128 | tf_op jit(solution)/shard_map/ppermute | solution.py:426
  37.8 0.7 add.6
  38.5 1.3 %collective-permute-start.4 = (f32[8,128]{1,0:T(8,128)S(1)}, f32[8,128]{1,0:T(8,128)S(1)}, u32[]{:S(2)}, u32[]{:S(2)}) collective-permute-start(f32[8,128]{1,0:T(8,128)S(1)} %add.6), channel_id=1, source_target_pairs={{0,2},{1,3},{2,0},{3,1},{4,6},{5,7},{6,4},{7,5},{8,10},{9,11},{10,... | collective-permute-start | bytes 12296 | tf_op jit(solution)/shard_map/ppermute | solution.py:426
  39.8 1.2 %collective-permute-done.4 = f32[8,128]{1,0:T(8,128)S(1)} collective-permute-done((f32[8,128]{1,0:T(8,128)S(1)}, f32[8,128]{1,0:T(8,128)S(1)}, u32[]{:S(2)}, u32[]{:S(2)}) %collective-permute-start.4) | collective-permute-done | bytes 4128 | tf_op jit(solution)/shard_map/ppermute | solution.py:426
  40.9 0.0 copy-start.11
  40.9 2.3 %collective-permute-start.5 = (f32[8,128]{1,0:T(8,128)S(1)}, f32[8,128]{1,0:T(8,128)S(1)}, u32[]{:S(2)}, u32[]{:S(2)}) collective-permute-start(f32[8,128]{1,0:T(8,128)S(1)} %add.7.mine), channel_id=1, source_target_pairs={{0,4},{1,5},{2,6},{3,7},{4,0},{5,1},{6,2},{7,3},{8,12},{9,13},{10,... | collective-permute-start | bytes 12296 | tf_op jit(solution)/shard_map/ppermute | solution.py:426
  43.2 1.0 %collective-permute-done.5.theirs = f32[8,128]{1,0:T(8,128)S(1)} collective-permute-done((f32[8,128]{1,0:T(8,128)S(1)}, f32[8,128]{1,0:T(8,128)S(1)}, u32[]{:S(2)}, u32[]{:S(2)}) %collective-permute-start.5) | collective-permute-done | bytes 4128 | tf_op jit(solution)/shard_map/ppermute | solution.py:426
  44.3 0.0 copy-start.12
  44.3 0.0 copy-done.11
  44.3 0.6 copy-done.12
  44.9 3.9 %solve.1 = (f32[3,8,128,128]{3,2,1,0:T(8,128)}, f32[3,2,128,128]{3,2,1,0:T(8,128)}, f32[3,2,128,128]{3,2,1,0:T(8,128)}) custom-call(s32[4,2]{1,0:T(4,128)} %copy.15.lev, f32[8,128]{1,0:T(8,128)} %copy-done.11, f32[8,128]{1,0:T(8,128)} %copy-done.12, f32[3,10,144,128]{3,2,1,0:T(8,128)} %get-tuple-element.29.zs, f32[3,8,136,128]{3,2,1,0:T(8,128)} %get-tuple-element.22.w), custom_call_target="tpu_custom_call" | custom-call | flops 2097152 | bytes 5898240 | tf_op jit(solution)/shard_map/solve/pallas_call | solution.py:521
  48.7 0.0 collective-permute-start.6
  48.7 2.4 %collective-permute-start.9 = (f32[3,2,128,128]{3,2,1,0:T(8,128)}, f32[3,2,128,128]{3,2,1,0:T(8,128)S(1)}, u32[]{:S(2)}, u32[]{:S(2)}) collective-permute-start(f32[3,2,128,128]{3,2,1,0:T(8,128)} %get-tuple-element.31), channel_id=1, source_target_pairs={{0,16},{8,24},{16,0},{24,8},{1,17},{9,25},{17,1},{25,9},{2,18},{10... | collective-permute-start | bytes 1179656 | tf_op jit(solution)/shard_map/ppermute | solution.py:426
  51.2 0.0 collective-permute-start.8
  51.2 0.5 collective-permute-start.7
  51.7 5.3 %collective-permute-done.6.refs_0_ = f32[3,2,128,128]{3,2,1,0:T(8,128)S(1)} collective-permute-done((f32[3,2,128,128]{3,2,1,0:T(8,128)}, f32[3,2,128,128]{3,2,1,0:T(8,128)S(1)}, u32[]{:S(2)}, u32[]{:S(2)}) %collective-permute-start.6) | collective-permute-done | bytes 393248 | tf_op jit(solution)/shard_map/ppermute | solution.py:426
  57.0 0.0 copy-start
  57.0 1.3 %collective-permute-start.10 = (f32[3,2,128,128]{3,2,1,0:T(8,128)S(1)}, f32[3,2,128,128]{3,2,1,0:T(8,128)S(1)}, u32[]{:S(2)}, u32[]{:S(2)}) collective-permute-start(f32[3,2,128,128]{3,2,1,0:T(8,128)S(1)} %collective-permute-done.6.refs_0_), channel_id=1, source_target_pairs={{0,16},{8,24},{16,0},{24,8},{1,17},{9,25},{17,1},{25,9},{2,18},{10... | collective-permute-start | bytes 1179656 | tf_op jit(solution)/shard_map/ppermute | solution.py:426
  58.2 0.0 collective-permute-done.9.refs_3_
  58.2 0.0 copy-start.1
  58.2 1.2 %collective-permute-start.11 = (f32[3,2,128,128]{3,2,1,0:T(8,128)S(1)}, f32[3,2,128,128]{3,2,1,0:T(8,128)S(1)}, u32[]{:S(2)}, u32[]{:S(2)}) collective-permute-start(f32[3,2,128,128]{3,2,1,0:T(8,128)S(1)} %collective-permute-done.9.refs_3_), channel_id=1, source_target_pairs={{0,8},{8,0},{16,24},{24,16},{1,9},{9,1},{17,25},{25,17},{2,10},{10... | collective-permute-start | bytes 1179656 | tf_op jit(solution)/shard_map/ppermute | solution.py:426
  59.4 7.0 %collective-permute-done.8.refs_2_ = f32[3,2,128,128]{3,2,1,0:T(8,128)S(1)} collective-permute-done((f32[3,2,128,128]{3,2,1,0:T(8,128)}, f32[3,2,128,128]{3,2,1,0:T(8,128)S(1)}, u32[]{:S(2)}, u32[]{:S(2)}) %collective-permute-start.8) | collective-permute-done | bytes 393248 | tf_op jit(solution)/shard_map/ppermute | solution.py:426
  66.4 0.0 copy-start.2
  66.4 0.0 collective-permute-done.7.refs_1_
  66.4 8.4 %collective-permute-done.10.refs_4_ = f32[3,2,128,128]{3,2,1,0:T(8,128)S(1)} collective-permute-done((f32[3,2,128,128]{3,2,1,0:T(8,128)S(1)}, f32[3,2,128,128]{3,2,1,0:T(8,128)S(1)}, u32[]{:S(2)}, u32[]{:S(2)}) %collective-permute-start.10) | collective-permute-done | bytes 393248 | tf_op jit(solution)/shard_map/ppermute | solution.py:426
  74.8 0.0 collective-permute-done.11.refs_5_
  74.8 0.0 copy-done
  74.8 0.0 copy-done.1
  74.8 0.0 copy-done.2
  74.8 0.0 copy-done.3
  74.9 0.7 copy-done.4
  75.6 0.8 copy-done.5
  76.3 2.4 %edges.1 = (f32[3,128,128]{2,1,0:T(8,128)}, f32[3,128,128]{2,1,0:T(8,128)}) custom-call(s32[4,2]{1,0:T(4,128)} %copy.15.lev, s32[4,3]{1,0:T(4,128)} %nb.3, f32[3,2,128,128]{3,2,1,0:T(8,128)} %copy-done, f32[3,2,128,128]{3,2,1,0:T(8,128)} %copy-done.3, f32[3,2,128,128]{3,2,1,0:T(8,128)} %copy-done.2, f32[3,2,128,128]{3,2,1,0:T(8,128)} %copy-done.1, ...), custom_call_target="tpu_custom_call" | custom-call | flops 6553600 | bytes 2621440 | tf_op jit(solution)/shard_map/edges/pallas_call | solution.py:532
  78.7 6.6 %collective-permute-start.12 = (f32[3,128,128]{2,1,0:T(8,128)}, f32[3,128,128]{2,1,0:T(8,128)S(1)}, u32[]{:S(2)}, u32[]{:S(2)}) collective-permute-start(f32[3,128,128]{2,1,0:T(8,128)} %get-tuple-element.32), channel_id=1, source_target_pairs={{0,1},{1,2},{2,3},{3,4},{4,5},{5,6},{6,7},{8,9},{9,10},{10,11},{11... | collective-permute-start | bytes 589832 | tf_op jit(solution)/shard_map/ppermute | solution.py:416
  85.3 1.9 %collective-permute-start.13 = (f32[3,128,128]{2,1,0:T(8,128)}, f32[3,128,128]{2,1,0:T(8,128)S(1)}, u32[]{:S(2)}, u32[]{:S(2)}) collective-permute-start(f32[3,128,128]{2,1,0:T(8,128)} %get-tuple-element.33), channel_id=1, source_target_pairs={{1,0},{2,1},{3,2},{4,3},{5,4},{6,5},{7,6},{9,8},{10,9},{11,10},{12... | collective-permute-start | bytes 589832 | tf_op jit(solution)/shard_map/ppermute | solution.py:421
  87.3 3.4 %mix.1.given = f32[3,8,128,128]{3,2,1,0:T(8,128)} custom-call(s32[4,2]{1,0:T(4,128)} %copy.15.lev, s32[4,3]{1,0:T(4,128)} %nb.3, f32[3,8,128,128]{3,2,1,0:T(8,128)} %get-tuple-element.34.u, f32[3,2,128,128]{3,2,1,0:T(8,128)} %copy-done, f32[3,2,128,128]{3,2,1,0:T(8,128)} %copy-done.3, f32[3,2,128,128]{3,2,1,0:T(8,128)} %copy-done.2, ...), custom_call_target="tpu_custom_call" | custom-call | flops 131072000 | bytes 5898240 | tf_op jit(solution)/shard_map/mix/pallas_call | solution.py:542
  90.6 0.0 collective-permute-done.12.lo
  90.6 1.9 %collective-permute-done.13.hi = f32[3,128,128]{2,1,0:T(8,128)S(1)} collective-permute-done((f32[3,128,128]{2,1,0:T(8,128)}, f32[3,128,128]{2,1,0:T(8,128)S(1)}, u32[]{:S(2)}, u32[]{:S(2)}) %collective-permute-start.13) | collective-permute-done | bytes 196640 | tf_op jit(solution)/shard_map/ppermute | solution.py:421
  92.5 0.0 copy-done.8
  92.5 0.7 copy-done.9
  93.2 2.8 %finish.1 = f32[3,8,128,128]{3,2,1,0:T(8,128)} custom-call(s32[4,2]{1,0:T(4,128)} %copy.15.lev, f32[3,128,128]{2,1,0:T(8,128)} %copy-done.8, f32[3,128,128]{2,1,0:T(8,128)} %copy-done.9, f32[3,8,128,128]{3,2,1,0:T(8,128)} %mix.1.given), custom_call_target="tpu_custom_call", output_to_operand_aliasing={{}: (3, {})} | custom-call | bytes 1179648 | tf_op jit(solution)/shard_map/finish/pallas_call | solution.py:551
  (6 shorter events, 0.0 us)
Async XLA Ops:
  1.3 9.6 %copy-start.13 = (f32[1,3,3]{2,0,1:T(1,128)S(1)}, f32[1,3,3]{2,0,1:T(1,128)}, u32[]{:S(2)}) copy-start(f32[1,3,3]{2,0,1:T(1,128)} %param.9) | copy-start | bytes 112
  1.4 9.6 %copy-start.14 = (f32[1,3,3]{2,0,1:T(1,128)S(1)}, f32[1,3,3]{2,0,1:T(1,128)}, u32[]{:S(2)}) copy-start(f32[1,3,3]{2,0,1:T(1,128)} %param.8) | copy-start | bytes 112
  4.4 10.3 %collective-permute-start = (f32[7,128,128]{2,1,0:T(8,128)}, f32[7,128,128]{2,1,0:T(8,128)S(1)}, u32[]{:S(2)}, u32[]{:S(2)}) collective-permute-start(f32[7,128,128]{2,1,0:T(8,128)} %get-tuple-element.20), channel_id=1, source_target_pairs={{0,1},{1,2},{2,3},{3,4},{4,5},{5,6},{6,7},{8,9},{9,10},{10,11},{11... | collective-permute-start | bytes 1376264 | tf_op jit(solution)/shard_map/ppermute | solution.py:416
  9.0 10.0 %collective-permute-start.1 = (f32[7,128,128]{2,1,0:T(8,128)}, f32[7,128,128]{2,1,0:T(8,128)S(1)}, u32[]{:S(2)}, u32[]{:S(2)}) collective-permute-start(f32[7,128,128]{2,1,0:T(8,128)} %get-tuple-element.21), channel_id=1, source_target_pairs={{1,0},{2,1},{3,2},{4,3},{5,4},{6,5},{7,6},{9,8},{10,9},{11,10},{12... | collective-permute-start | bytes 1376264 | tf_op jit(solution)/shard_map/ppermute | solution.py:421
  14.7 4.3 %copy-start.6 = (f32[7,128,128]{2,1,0:T(8,128)}, f32[7,128,128]{2,1,0:T(8,128)S(1)}, u32[]{:S(2)}) copy-start(f32[7,128,128]{2,1,0:T(8,128)S(1)} %collective-permute-done.lo) | copy-start | bytes 1376260
  19.0 0.8 copy-start.7
  27.9 5.5 %collective-permute-start.2 = (f32[3,128,128]{2,1,0:T(8,128)}, f32[3,128,128]{2,1,0:T(8,128)S(1)}, u32[]{:S(2)}, u32[]{:S(2)}) collective-permute-start(f32[3,128,128]{2,1,0:T(8,128)} %get-tuple-element.24), channel_id=1, source_target_pairs={{0,1},{1,2},{2,3},{3,4},{4,5},{5,6},{6,7},{8,9},{9,10},{10,11},{11... | collective-permute-start | bytes 589832 | tf_op jit(solution)/shard_map/ppermute | solution.py:416
  33.4 0.7 copy-start.10
  36.2 1.5 %collective-permute-start.3 = (f32[8,128]{1,0:T(8,128)}, f32[8,128]{1,0:T(8,128)S(1)}, u32[]{:S(2)}, u32[]{:S(2)}) collective-permute-start(f32[8,128]{1,0:T(8,128)} %cross.1), channel_id=1, source_target_pairs={{0,1},{1,0},{2,3},{3,2},{4,5},{5,4},{6,7},{7,6},{8,9},{9,8},{10,11... | collective-permute-start | bytes 12296 | tf_op jit(solution)/shard_map/ppermute | solution.py:426
  38.5 2.5 %collective-permute-start.4 = (f32[8,128]{1,0:T(8,128)S(1)}, f32[8,128]{1,0:T(8,128)S(1)}, u32[]{:S(2)}, u32[]{:S(2)}) collective-permute-start(f32[8,128]{1,0:T(8,128)S(1)} %add.6), channel_id=1, source_target_pairs={{0,2},{1,3},{2,0},{3,1},{4,6},{5,7},{6,4},{7,5},{8,10},{9,11},{10,... | collective-permute-start | bytes 12296 | tf_op jit(solution)/shard_map/ppermute | solution.py:426
  40.9 3.4 %copy-start.11 = (f32[8,128]{1,0:T(8,128)}, f32[8,128]{1,0:T(8,128)S(1)}, u32[]{:S(2)}) copy-start(f32[8,128]{1,0:T(8,128)S(1)} %add.7.mine) | copy-start | bytes 12292
  40.9 3.4 %collective-permute-start.5 = (f32[8,128]{1,0:T(8,128)S(1)}, f32[8,128]{1,0:T(8,128)S(1)}, u32[]{:S(2)}, u32[]{:S(2)}) collective-permute-start(f32[8,128]{1,0:T(8,128)S(1)} %add.7.mine), channel_id=1, source_target_pairs={{0,4},{1,5},{2,6},{3,7},{4,0},{5,1},{6,2},{7,3},{8,12},{9,13},{10,... | collective-permute-start | bytes 12296 | tf_op jit(solution)/shard_map/ppermute | solution.py:426
  44.3 0.6 copy-start.12
  48.7 8.2 %collective-permute-start.6 = (f32[3,2,128,128]{3,2,1,0:T(8,128)}, f32[3,2,128,128]{3,2,1,0:T(8,128)S(1)}, u32[]{:S(2)}, u32[]{:S(2)}) collective-permute-start(f32[3,2,128,128]{3,2,1,0:T(8,128)} %get-tuple-element.30), channel_id=1, source_target_pairs={{0,8},{8,0},{16,24},{24,16},{1,9},{9,1},{17,25},{25,17},{2,10},{10... | collective-permute-start | bytes 1179656 | tf_op jit(solution)/shard_map/ppermute | solution.py:426
  48.7 9.5 %collective-permute-start.9 = (f32[3,2,128,128]{3,2,1,0:T(8,128)}, f32[3,2,128,128]{3,2,1,0:T(8,128)S(1)}, u32[]{:S(2)}, u32[]{:S(2)}) collective-permute-start(f32[3,2,128,128]{3,2,1,0:T(8,128)} %get-tuple-element.31), channel_id=1, source_target_pairs={{0,16},{8,24},{16,0},{24,8},{1,17},{9,25},{17,1},{25,9},{2,18},{10... | collective-permute-start | bytes 1179656 | tf_op jit(solution)/shard_map/ppermute | solution.py:426
  51.2 15.2 %collective-permute-start.8 = (f32[3,2,128,128]{3,2,1,0:T(8,128)}, f32[3,2,128,128]{3,2,1,0:T(8,128)S(1)}, u32[]{:S(2)}, u32[]{:S(2)}) collective-permute-start(f32[3,2,128,128]{3,2,1,0:T(8,128)} %get-tuple-element.30), channel_id=1, source_target_pairs={{0,16},{8,24},{16,0},{24,8},{1,17},{9,25},{17,1},{25,9},{2,18},{10... | collective-permute-start | bytes 1179656 | tf_op jit(solution)/shard_map/ppermute | solution.py:426
  51.2 15.2 %collective-permute-start.7 = (f32[3,2,128,128]{3,2,1,0:T(8,128)}, f32[3,2,128,128]{3,2,1,0:T(8,128)S(1)}, u32[]{:S(2)}, u32[]{:S(2)}) collective-permute-start(f32[3,2,128,128]{3,2,1,0:T(8,128)} %get-tuple-element.31), channel_id=1, source_target_pairs={{0,8},{8,0},{16,24},{24,16},{1,9},{9,1},{17,25},{25,17},{2,10},{10... | collective-permute-start | bytes 1179656 | tf_op jit(solution)/shard_map/ppermute | solution.py:426
  57.0 17.8 %copy-start = (f32[3,2,128,128]{3,2,1,0:T(8,128)}, f32[3,2,128,128]{3,2,1,0:T(8,128)S(1)}, u32[]{:S(2)}) copy-start(f32[3,2,128,128]{3,2,1,0:T(8,128)S(1)} %collective-permute-done.6.refs_0_) | copy-start | bytes 1179652
  57.0 17.8 %collective-permute-start.10 = (f32[3,2,128,128]{3,2,1,0:T(8,128)S(1)}, f32[3,2,128,128]{3,2,1,0:T(8,128)S(1)}, u32[]{:S(2)}, u32[]{:S(2)}) collective-permute-start(f32[3,2,128,128]{3,2,1,0:T(8,128)S(1)} %collective-permute-done.6.refs_0_), channel_id=1, source_target_pairs={{0,16},{8,24},{16,0},{24,8},{1,17},{9,25},{17,1},{25,9},{2,18},{10... | collective-permute-start | bytes 1179656 | tf_op jit(solution)/shard_map/ppermute | solution.py:426
  58.2 16.6 %copy-start.1 = (f32[3,2,128,128]{3,2,1,0:T(8,128)}, f32[3,2,128,128]{3,2,1,0:T(8,128)S(1)}, u32[]{:S(2)}) copy-start(f32[3,2,128,128]{3,2,1,0:T(8,128)S(1)} %collective-permute-done.9.refs_3_) | copy-start | bytes 1179652
  58.2 16.6 %collective-permute-start.11 = (f32[3,2,128,128]{3,2,1,0:T(8,128)S(1)}, f32[3,2,128,128]{3,2,1,0:T(8,128)S(1)}, u32[]{:S(2)}, u32[]{:S(2)}) collective-permute-start(f32[3,2,128,128]{3,2,1,0:T(8,128)S(1)} %collective-permute-done.9.refs_3_), channel_id=1, source_target_pairs={{0,8},{8,0},{16,24},{24,16},{1,9},{9,1},{17,25},{25,17},{2,10},{10... | collective-permute-start | bytes 1179656 | tf_op jit(solution)/shard_map/ppermute | solution.py:426
  66.4 8.4 %copy-start.2 = (f32[3,2,128,128]{3,2,1,0:T(8,128)}, f32[3,2,128,128]{3,2,1,0:T(8,128)S(1)}, u32[]{:S(2)}) copy-start(f32[3,2,128,128]{3,2,1,0:T(8,128)S(1)} %collective-permute-done.8.refs_2_) | copy-start | bytes 1179652
  66.4 8.5 %copy-start.3 = (f32[3,2,128,128]{3,2,1,0:T(8,128)}, f32[3,2,128,128]{3,2,1,0:T(8,128)S(1)}, u32[]{:S(2)}) copy-start(f32[3,2,128,128]{3,2,1,0:T(8,128)S(1)} %collective-permute-done.7.refs_1_) | copy-start | bytes 1179652
  74.8 0.8 copy-start.4
  75.6 0.8 copy-start.5
  78.7 11.9 %collective-permute-start.12 = (f32[3,128,128]{2,1,0:T(8,128)}, f32[3,128,128]{2,1,0:T(8,128)S(1)}, u32[]{:S(2)}, u32[]{:S(2)}) collective-permute-start(f32[3,128,128]{2,1,0:T(8,128)} %get-tuple-element.32), channel_id=1, source_target_pairs={{0,1},{1,2},{2,3},{3,4},{4,5},{5,6},{6,7},{8,9},{9,10},{10,11},{11... | collective-permute-start | bytes 589832 | tf_op jit(solution)/shard_map/ppermute | solution.py:416
  85.3 7.2 %collective-permute-start.13 = (f32[3,128,128]{2,1,0:T(8,128)}, f32[3,128,128]{2,1,0:T(8,128)S(1)}, u32[]{:S(2)}, u32[]{:S(2)}) collective-permute-start(f32[3,128,128]{2,1,0:T(8,128)} %get-tuple-element.33), channel_id=1, source_target_pairs={{1,0},{2,1},{3,2},{4,3},{5,4},{6,5},{7,6},{9,8},{10,9},{11,10},{12... | collective-permute-start | bytes 589832 | tf_op jit(solution)/shard_map/ppermute | solution.py:421
  90.6 1.9 %copy-start.8 = (f32[3,128,128]{2,1,0:T(8,128)}, f32[3,128,128]{2,1,0:T(8,128)S(1)}, u32[]{:S(2)}) copy-start(f32[3,128,128]{2,1,0:T(8,128)S(1)} %collective-permute-done.12.lo) | copy-start | bytes 589828
  92.5 0.7 copy-start.9

commit v2 on v1

v2 whole, which is shorter than its diff:
```python
import functools

import jax
import jax.numpy as jnp
from jax import lax
from jax.experimental import pallas as pl
from jax.experimental.pallas import tpu as pltpu
from jax.sharding import PartitionSpec as P

CHUNK = 32
PAD = 8
VMEM_SPEC = pl.BlockSpec(memory_space=pltpu.VMEM)
SMEM_SPEC = pl.BlockSpec(memory_space=pltpu.SMEM)
HBM_SPEC = pl.BlockSpec(memory_space=pltpu.HBM)
VMEM_LIMIT = 18 * 1024 * 1024
f32 = jnp.float32


def shape_of(*dims):
    return jax.ShapeDtypeStruct(dims, f32)


def estimate(flops, nbytes):
    return pl.CostEstimate(flops=int(flops), bytes_accessed=int(nbytes), transcendentals=0)


def cells(full, level):
    return lax.shift_right_logical(jnp.int32(full), 2 - level)


def lanes(rows, width):
    return lax.broadcasted_iota(jnp.int32, (rows, width), 1)


def coefficients(an, nx, nz, height):
    wx = nx.astype(f32) / height
    wz = nz.astype(f32) / height
    wx, wz = wx * wx, wz * wz
    return [[an[c, 0, 0] * wx, an[c, 0, 1], an[c, 0, 2] * wz] for c in range(3)]


def fold(values):
    rows = values.shape[0]
    total = values[0:8]
    for start in range(8, rows, 8):
        total = total + values[start : start + 8]
    return total


def rims_kernel(lev, f_hbm, k_hbm, one, two, sems):
    depth = f_hbm.shape[1]
    a = cells(depth, lev[1, lax.axis_index("grp")])
    even = lax.rem(lax.axis_index("slab"), 2) == 0
    started = []
    for i, (rows, last) in enumerate(((one, even), (two, jnp.logical_not(even)))):
        near = jnp.where(last, a - 1, 0)
        far = jnp.where(last, a - 2, 1)
        for j, (source, target) in enumerate(
            (
                (f_hbm.at[:, near], rows.at[0:3]),
                (k_hbm.at[:, near], rows.at[3:6]),
                (k_hbm.at[2, far], rows.at[6]),
            )
        ):
            started.append(pltpu.make_async_copy(source, target, sems.at[3 * i + j]))
    for copy in started:
        copy.start()
    for copy in started:
        copy.wait()


def first_kernel(
    slabs, lev, an, cp, f, k, one, two, zs, w, wl, w0, gx, gys, gz, gl, dots, rj, kys, kzs
):
    _, depth, height, width = f.shape
    g = lax.axis_index("grp")
    nx = cells(width, lev[0, g])
    a = cells(depth, lev[1, g])
    co = coefficients(an, nx, a * slabs, height)
    lane = lanes(CHUNK, width)
    in_x = lane < nx
    in_xp = lane < nx - 1
    in_xm = lane > 0
    chunks = range(0, height, CHUNK)
    zero_pad = jnp.zeros((PAD, width), f32)

    def keep(values):
        return jnp.where(in_x, values, 0.0)

    def pad_row(row):
        kys[row, 0:PAD] = zero_pad
        kys[row, height + PAD :] = zero_pad
        for c in range(3):
            zs[c, row, 0:PAD] = zero_pad
            zs[c, row, height + PAD :] = zero_pad

    def stage(row, _):
        pad_row(row + 1)
        for y in chunks:
            kys[row + 1, PAD + y : PAD + y + CHUNK] = keep(k[1, row, y : y + CHUNK])
            kzs[row + 2, y : y + CHUNK] = keep(k[2, row, y : y + CHUNK])
        return 0

    lax.fori_loop(0, a, stage, 0)
    pad_row(0)
    pad_row(a + 1)
    even = lax.rem(lax.axis_index("slab"), 2) == 0
    rims = []
    for rows, above in ((one, even), (two, jnp.logical_not(even))):
        at = jnp.where(above, a + 1, 0)
        near = jnp.where(above, a + 2, 1)
        far = jnp.where(above, a + 3, 0)
        rims.append((rows, at))
        for y in chunks:
            here = slice(y, y + CHUNK)
            kys[at, PAD + y : PAD + y + CHUNK] = keep(rows[4, here])
            kzs[near, here] = keep(rows[5, here])
            kzs[far, here] = keep(rows[6, here])

    def jacobi(f_at, kx_at, row, own):
        for y in chunks:
            kx = keep(kx_at(y))
            kxp = jnp.where(in_xp, pltpu.roll(kx, width - 1, 1), 0.0)
            kxm = jnp.where(in_xm, pltpu.roll(kx, 1, 1), 0.0)
            ky = kys[row, PAD + y : PAD + y + CHUNK]
            kyp = kys[row, PAD + y + 1 : PAD + y + 1 + CHUNK]
            kym = kys[row, PAD + y - 1 : PAD + y - 1 + CHUNK]
            kz = kzs[row + 1, y : y + CHUNK]
            kzp = kzs[row + 2, y : y + CHUNK]
            kzm = kzs[row, y : y + CHUNK]
            sx = kx + 0.5 * (kxp + kxm)
            sy = ky + 0.5 * (kyp + kym)
            sz = kz + 0.5 * (kzp + kzm)
            for c in range(3):
                diagonal = cp[c, 0, c] + co[c][0] * sx + co[c][1] * sy + co[c][2] * sz
                inverse = 1.0 / diagonal
                zs[c, row, PAD + y : PAD + y + CHUNK] = keep(f_at(c, y)) * inverse
                if own:
                    rj[c, row - 1, y : y + CHUNK] = inverse
            if own:
                gx[row - 1, y : y + CHUNK] = jnp.where(in_xp, 0.5 * (kx + kxp), 0.0)
                gys[row - 1, PAD + y : PAD + y + CHUNK] = 0.5 * (ky + kyp)
                gz[row - 1, y : y + CHUNK] = 0.5 * (kz + kzp)

    def own_row(row, _):
        gys[row, 0:PAD] = zero_pad
        jacobi(
            lambda c, y: f[c, row, y : y + CHUNK], lambda y: k[0, row, y : y + CHUNK], row + 1, True
        )
        return 0

    for rows, at in rims:
        jacobi(
            lambda c, y: rows[c, y : y + CHUNK], lambda y: rows[3, y : y + CHUNK], at, False
        )
    lax.fori_loop(0, a, own_row, 0)
    for y in chunks:
        gl[y : y + CHUNK] = 0.5 * (kzs[1, y : y + CHUNK] + kzs[2, y : y + CHUNK])

    def image_row(row, sums):
        s0, s1, s2 = sums
        for c in range(3):
            w[c, row, height:] = zero_pad
        for y in chunks:
            here = slice(y, y + CHUNK)
            mid = slice(PAD + y, PAD + y + CHUNK)
            above = slice(PAD + y + 1, PAD + y + 1 + CHUNK)
            below = slice(PAD + y - 1, PAD + y - 1 + CHUNK)
            fx = gx[row, here]
            fyp, fym = gys[row, mid], gys[row, below]
            fzp = gz[row, here]
            fzm = 0.5 * (kzs[row + 1, here] + kzs[row + 2, here])
            z = [zs[c, row + 1, mid] for c in range(3)]
            for c in range(3):
                tx = fx * pltpu.roll(z[c], width - 1, 1) + pltpu.roll(fx * z[c], 1, 1)
                ty = fyp * zs[c, row + 1, above] + fym * zs[c, row + 1, below]
                tz = fzp * zs[c, row + 2, mid] + fzm * zs[c, row, mid]
                v = co[c][0] * tx + co[c][1] * ty + co[c][2] * tz
                for other in range(3):
                    if other != c:
                        v = v - cp[c, 0, other] * z[other]
                force = keep(f[c, row, here])
                image = force - v
                scaled = z[c] - v * rj[c, row, here]
                w[c, row, here] = scaled
                s0 = s0 + fold(force * z[c])
                s1 = s1 + fold(image * z[c])
                s2 = s2 + fold(image * scaled)
        return s0, s1, s2

    nothing = jnp.zeros((8, width), f32)
    s0, s1, s2 = lax.fori_loop(0, a, image_row, (nothing, nothing, nothing))
    for c in range(3):
        for y in chunks:
            wl[c, y : y + CHUNK] = w[c, a - 1, y : y + CHUNK]
            w0[c, y : y + CHUNK] = w[c, 0, y : y + CHUNK]
    dots[...] = jnp.zeros((8, width), f32)
    for i, total in enumerate((s0, s1, s2)):
        dots[i : i + 1, :] = jnp.sum(total, axis=0, keepdims=True)


def second_kernel(slabs, lev, an, cp, w, gx, gys, gz, part):
    depth, height, width = gx.shape
    g = lax.axis_index("grp")
    nx = cells(width, lev[0, g])
    a = cells(depth, lev[1, g])
    co = coefficients(an, nx, a * slabs, height)

    def row_sum(row, total, inner):
        for y in range(0, height, CHUNK):
            here = slice(y, y + CHUNK)
            fx, fy = gx[row, here], gys[row, PAD + y : PAD + y + CHUNK]
            fz = gz[row, here] if inner else None
            own = [w[c, row, here] for c in range(3)]
            for c in range(3):
                v = co[c][0] * (fx * pltpu.roll(own[c], width - 1, 1))
                v = v + co[c][1] * (fy * w[c, row, y + 1 : y + 1 + CHUNK])
                if inner:
                    v = v + co[c][2] * (fz * w[c, row + 1, here])
                if c < 2:
                    v = v - cp[c, 0, c + 1] * own[c + 1]
                if c == 0:
                    v = v - cp[0, 0, 2] * own[2]
                total = total + fold(v * own[c])
        return total

    total = lax.fori_loop(
        0, a - 1, lambda row, t: row_sum(row, t, True), jnp.zeros((8, width), f32)
    )
    part[...] = 2.0 * row_sum(a - 1, total, False)


def cross_kernel(slabs, depth, lev, an, w0, gl, wlo, part, dots, out):
    height, width = gl.shape
    g = lax.axis_index("grp")
    nx = cells(width, lev[0, g])
    a = cells(depth, lev[1, g])
    co = coefficients(an, nx, a * slabs, height)
    total = jnp.zeros((8, width), f32)
    for y in range(0, height, CHUNK):
        here = slice(y, y + CHUNK)
        v = jnp.zeros((CHUNK, width), f32)
        for c in range(3):
            v = v + co[c][2] * (w0[c, here] * wlo[c, here])
        total = total + fold(gl[here] * v)
    out[...] = dots[...]
    out[3:4, :] = jnp.sum(part[...] + 2.0 * total, axis=0, keepdims=True)


def slot_rows(depth, run):
    half, quarter = depth // 2, depth // 4
    last = jnp.where(run == quarter, quarter - 1, half - 1)
    rest = [n for n in range(1, half - 1) if n != quarter - 1]
    return [0, last] + rest + [half + quarter - 2 - last]


def solution_kernel(lev, mine, theirs, zs, w, u, *slots):
    _, depth, height, width = u.shape
    half = depth // 2
    g = lax.axis_index("grp")
    a = cells(depth, lev[1, g])
    narrow = lev[0, g] < 2
    sums = jnp.sum(mine[...] + theirs[...], axis=1, keepdims=True)
    sums = jnp.broadcast_to(sums, (8, width))
    d0, d1, d2, e3 = sums[0:1], sums[1:2], sums[2:3], sums[3:4]
    d3 = d2 - e3
    first = d0 / d1
    rz = first * first * d2 - d0
    more = 1.0 + rz / d0
    bend = more * more * d1 - 2.0 * first * more * d2 + first * first * d3
    second = rz / bend
    alpha = jnp.broadcast_to(first + second * more, (CHUNK, width))
    beta = jnp.broadcast_to(-second * first, (CHUNK, width))
    chunks = range(0, height, CHUNK)

    def active_row(row, _):
        for c in range(3):
            for y in chunks:
                z = zs[c, row + 1, PAD + y : PAD + y + CHUNK]
                u[c, row, y : y + CHUNK] = alpha * z + beta * w[c, row, y : y + CHUNK]
        return 0

    def idle_row(row, _):
        for c in range(3):
            for y in chunks:
                u[c, row, y : y + CHUNK] = jnp.zeros((CHUNK, width), f32)
        return 0

    lax.fori_loop(0, a, active_row, 0)
    lax.fori_loop(a, depth, idle_row, 0)
    share = jnp.where(narrow, 1.0, 0.0)
    for slot, n in zip(slots, slot_rows(depth, a)):
        for c in range(3):
            for y in chunks:
                here = slice(y, y + CHUNK)
                beside = pltpu.roll(u[c, n + half, here], width // 2, 1)
                slot[c, here] = u[c, n, here] + share * beside


def role(lev, nb, g, p):
    n0, n1, n2 = nb[g, 0], nb[g, 1], nb[g, 2]
    sign = jnp.where(n2 == p, 1.0, 0.0) - jnp.where((n0 == p) | (n1 == p), 1.0, 0.0)
    coarse = lev[1, p] < lev[1, g]
    return sign.astype(f32), coarse


def x_weights(lev, g, p, sign, width):
    to_x = cells(width, lev[0, g])
    from_x = cells(width, lev[0, p])
    source = lax.broadcasted_iota(jnp.int32, (width, 2 * width), 0)
    target = lax.broadcasted_iota(jnp.int32, (width, 2 * width), 1)
    second = target >= width
    target = jnp.where(second, target - width, target)
    shift = jnp.where(second, width // 2, 0)
    cell = source - shift
    ratio = from_x.astype(f32) / to_x.astype(f32)
    along = (target.astype(f32) + 0.5) * ratio
    weight = jnp.maximum(0.0, 1.0 - jnp.abs(along - (cell.astype(f32) + 0.5)))
    fits = (target < to_x) & (cell >= 0) & (cell < from_x)
    fits = fits & (jnp.logical_not(second) | (lev[0, p] < 2))
    return jnp.where(fits, weight * sign, 0.0).astype(jnp.bfloat16)


def split_dot(values, weights):
    high = values.astype(jnp.bfloat16)
    rest = values - high.astype(f32)
    middle = rest.astype(jnp.bfloat16)
    low = (rest - middle.astype(f32)).astype(jnp.bfloat16)
    dot = functools.partial(jnp.dot, preferred_element_type=f32)
    return dot(high, weights) + (dot(middle, weights) + dot(low, weights))


def edges_kernel(others, lev, nb, *refs):
    pieces = refs[: 2 * len(others)]
    one, two, weights = refs[2 * len(others) :]
    width = one.shape[2]
    g = lax.axis_index("grp")
    even = lax.rem(lax.axis_index("slab"), 2) == 0
    one[...] = jnp.zeros(one.shape, f32)
    two[...] = jnp.zeros(two.shape, f32)
    for i, other in enumerate(others):
        first, last = pieces[2 * i : 2 * i + 2]
        p = other(g)
        sign, coarse = role(lev, nb, g, p)

        @pl.when((sign != 0.0) & coarse)
        def _():
            weights[...] = x_weights(lev, g, p, sign, width)[:, :width]

            def component(c, _):
                below = 0.25 * split_dot(first[c], weights[...])
                above = 0.25 * split_dot(last[c], weights[...])
                one[c] += jnp.where(even, above, below)
                two[c] += jnp.where(even, below, above)
                return 0

            lax.fori_loop(0, 3, component, 0)


def mix_kernel(others, which, depth, ends, lev, nb, start, *refs):
    pieces = refs[: len(which) * len(others)]
    rims = refs[len(pieces) : len(pieces) + (2 if ends else 0)]
    out, weights = refs[len(pieces) + len(rims) :]
    width = start.shape[3]
    half = depth // 2
    g = lax.axis_index("grp")
    run = cells(depth, lev[1, g])

    def begin(c, _):
        for row in range(depth):
            out[c, row] = start[c, row]
        return 0

    lax.fori_loop(0, 3, begin, 0)
    for i, other in enumerate(others):
        p = other(g)
        sign, coarse = role(lev, nb, g, p)
        slots = pieces[len(which) * i : len(which) * (i + 1)]
        order = slot_rows(depth, cells(depth, lev[1, p]))
        rows = [order[j] for j in which]

        @pl.when(sign != 0.0)
        def _():
            weights[...] = x_weights(lev, g, p, sign, width)

        @pl.when((sign != 0.0) & jnp.logical_not(coarse))
        def _():
            def component(c, _):
                for n, slot in zip(rows, slots):
                    both = split_dot(slot[c], weights[...])
                    out[c, n] += both[:, :width]
                    out[c, n + half] += both[:, width:]
                return 0

            lax.fori_loop(0, 3, component, 0)

        @pl.when((sign != 0.0) & coarse)
        def _():
            def component(c, _):
                for n, slot in zip(rows, slots):
                    one = split_dot(slot[c], weights[:, :width])
                    out[c, 2 * n] += 0.75 * one
                    out[c, 2 * n + 1] += 0.75 * one
                    before = jnp.where(n > 0, 0.25, 0.0)
                    after = jnp.where(2 * n + 2 < run, 0.25, 0.0)
                    out[c, jnp.maximum(2 * n - 1, 0)] += before * one
                    out[c, jnp.minimum(2 * n + 2, depth - 1)] += after * one
                return 0

            lax.fori_loop(0, 3, component, 0)

    if ends:
        even = lax.rem(lax.axis_index("slab"), 2) == 0
        for rim, above in zip(rims, (even, jnp.logical_not(even))):
            row = jnp.where(above, run - 1, 0)
            for c in range(3):
                out[c, row] += rim[c]


def permute_up(values):
    slabs = lax.axis_size("slab")
    return lax.ppermute(values, "slab", [(i, i + 1) for i in range(slabs - 1)])


def exchange(one, two):
    slabs = lax.axis_size("slab")
    pairs = [(i, i + 1) for i in range(1, slabs - 1, 2)]
    other = lax.ppermute(two, "slab", pairs + [(j, i) for i, j in pairs])
    return along(one, "slab", 1), other


def along(values, axis, step):
    peers = lax.axis_size(axis)
    return lax.ppermute(values, axis, [(i, i ^ step) for i in range(peers)])


def slab_sums(sums):
    slabs = lax.axis_size("slab")
    step = 1
    while 2 * step < slabs:
        sums = sums + along(sums, "slab", step)
        step *= 2
    return sums, along(sums, "slab", step)


def gather(slots):
    groups = lax.axis_size("grp")
    if groups != 4:
        return [[along(slot, "grp", step) for slot in slots] for step in range(1, groups)]
    by_x, by_y, by_both = {}, {}, {}
    for i in range(0, len(slots), 2):
        j = i + 1
        by_x[i], by_y[j] = along(slots[i], "grp", 1), along(slots[j], "grp", 2)
        by_x[j], by_y[i] = along(slots[j], "grp", 1), along(slots[i], "grp", 2)
        by_both[i], by_both[j] = along(by_x[i], "grp", 2), along(by_y[j], "grp", 1)
    return [[group[i] for i in range(len(slots))] for group in (by_x, by_y, by_both)]


def call(kernel, outs, specs_in, specs_out, scratch=(), cost=None, limit=VMEM_LIMIT, **more):
    return pl.pallas_call(
        kernel,
        out_shape=outs,
        in_specs=specs_in,
        out_specs=specs_out,
        scratch_shapes=list(scratch),
        cost_estimate=cost,
        compiler_params=pltpu.CompilerParams(vmem_limit_bytes=limit),
        **more,
    )


def per_device(forcing, stiffness, anisotropy, coupling, levels, neighbours):
    _, _, depth, height, width = forcing.shape
    slabs = lax.axis_size("slab")
    f, k = forcing[0], stiffness[0]
    levels = levels.T
    an = jnp.transpose(anisotropy, (1, 0, 2))
    cp = jnp.transpose(coupling, (1, 0, 2))
    plane = 4 * height * width
    padded = height + 2 * PAD
    rows3 = shape_of(3, height, width)
    whole = shape_of(3, depth, height, width)

    one, two = call(
        rims_kernel,
        [shape_of(7, height, width)] * 2,
        [SMEM_SPEC, HBM_SPEC, HBM_SPEC],
        [VMEM_SPEC] * 2,
        [pltpu.SemaphoreType.DMA((6,))],
        estimate(0, 28 * plane),
        limit=60 * 1024 * 1024,
        name="rims",
    )(levels, f, k)
    one, two = exchange(one, two)

    zs, w, wl, w0, gx, gys, gz, gl, dots = call(
        functools.partial(first_kernel, slabs),
        [
            shape_of(3, depth + 2, padded, width),
            shape_of(3, depth, height + PAD, width),
            rows3,
            rows3,
            shape_of(depth, height, width),
            shape_of(depth, height + PAD, width),
            shape_of(depth, height, width),
            shape_of(height, width),
            shape_of(8, width),
        ],
        [SMEM_SPEC] * 3 + [VMEM_SPEC] * 4,
        [VMEM_SPEC] * 9,
        [
            pltpu.VMEM((3, depth, height, width), f32),
            pltpu.VMEM((depth + 2, padded, width), f32),
            pltpu.VMEM((depth + 4, height, width), f32),
        ],
        estimate(150 * depth * plane, 150 * plane),
        name="first",
    )(levels, an, cp, f, k, one, two)
    wlo = permute_up(wl)
    part = call(
        functools.partial(second_kernel, slabs),
        shape_of(8, width),
        [SMEM_SPEC] * 3 + [VMEM_SPEC] * 4,
        VMEM_SPEC,
        cost=estimate(30 * depth * plane, 50 * plane),
        name="second",
    )(levels, an, cp, w, gx, gys, gz)
    dots = call(
        functools.partial(cross_kernel, slabs, depth),
        shape_of(8, width),
        [SMEM_SPEC] * 2 + [VMEM_SPEC] * 5,
        VMEM_SPEC,
        cost=estimate(8 * plane, 6 * plane),
        name="cross",
    )(levels, an, w0, gl, wlo, part, dots)
    mine, theirs = slab_sums(dots)
    half = depth // 2
    u, *slots = call(
        solution_kernel,
        [whole] + [rows3] * half,
        [SMEM_SPEC] + [VMEM_SPEC] * 4,
        [VMEM_SPEC] * (1 + half),
        cost=estimate(4 * depth * plane, 90 * plane),
        name="solve",
    )(levels, mine, theirs, zs, w)
    received = gather(slots)
    steps = range(1, len(received) + 1)
    others = [functools.partial(lambda step, g: g ^ step, step) for step in steps]
    early = [slot for group in received for slot in group[:2]]
    edge_one, edge_two = call(
        functools.partial(edges_kernel, others),
        [rows3] * 2,
        [SMEM_SPEC] * 2 + [VMEM_SPEC] * len(early),
        [VMEM_SPEC] * 2,
        [pltpu.VMEM((width, width), jnp.bfloat16)],
        estimate(100 * plane, 40 * plane),
        name="edges",
    )(levels, neighbours, *early)
    rims = exchange(edge_one, edge_two)

    def mix(start, members, which, ends, name):
        pieces = [received[i][j] for i in members for j in which]
        given = pieces + (list(rims) if ends else [])
        return call(
            functools.partial(mix_kernel, [others[i] for i in members], which, depth, ends),
            whole,
            [SMEM_SPEC] * 2 + [VMEM_SPEC] * (1 + len(given)),
            VMEM_SPEC,
            [pltpu.VMEM((width, 2 * width), jnp.bfloat16)],
            estimate(1000 * plane, (48 + 3 * len(given)) * plane),
            input_output_aliases={} if ends else {2: 0},
            name=name,
        )(levels, neighbours, start, *given)

    members = list(range(len(received)))
    mixed = mix(u, members, range(2), False, "mix_one")
    mixed = mix(mixed, members[:-1], range(2, half), False, "mix_two")
    mixed = mix(mixed, members[-1:], range(2, half), True, "mix_three")
    return mixed[None]


def solution(mesh):
    return jax.shard_map(
        per_device,
        mesh=mesh,
        in_specs=(
            P("grp", None, "slab", None, None),
            P("grp", None, "slab", None, None),
            P("grp", None, None),
            P("grp", None, None),
            P(),
            P(),
        ),
        out_specs=P("grp", None, "slab", None, None),
        check_vma=False,
    )
```

time: 96.5 us -> 70.7 us (0.73)
  waiting for transfers between devices: 33.3 us -> 18.5 us
  Pallas kernels: 29.4 us -> 19.1 us
  starting transfers between devices: 26.4 us -> 33.2 us
  local copies, waits for them, and re-layouts: 6.14 us -> 0.02 us
    ppermute x9 -> x17, waiting for transfers between devices: 23.9 us -> 11.2 us  [along(): return lax.ppermute(values, axis, [(i, i ^ step) for i in range(peers)])]
    ppermute x9 -> x17, starting transfers between devices: 9.51 us -> 21.2 us  [along(): return lax.ppermute(values, axis, [(i, i ^ step) for i in range(peers)])]
    ppermute x3 -> x1, starting transfers between devices: 13.1 us -> 3.65 us  [permute_up(): return lax.ppermute(values, 'slab', [(i, i + 1) for i in range(slabs - 1)])]
    unnamed x32 -> x12, local copies, waits for them, and re-layouts: 6.14 us -> 0.02 us
    pallas_call x6 -> x7, Pallas kernels: 17.7 us -> 13.1 us  [the longest x3 6.85 us: mix(): call(functools.partial(mix_kernel, [others[i] for i in members], which, d...]
    ppermute x2, starting transfers between devices: 3.84 us -> 8.32 us  [exchange(): other = lax.ppermute(two, 'slab', pairs + [(j, i) for i, j in pairs])]
    pallas_call x1, Pallas kernels: 8.15 us -> 4.21 us  [per_device(): call(functools.partial(first_kernel, slabs), [shape_of(3, depth + 2, padd...]
    ppermute x3 -> x1, waiting for transfers between devices: 3.19 us -> 0.87 us  [permute_up(): return lax.ppermute(values, 'slab', [(i, i + 1) for i in range(slabs - 1)])]
  transfers between devices with their start and end apart: 14 -> 20, of which waited for: 9 -> 10; matrix products, arithmetic and copies ran while one was open for 1% -> 0% of each run, Pallas kernels for 7% -> 11%
where the time goes in v2:
time: 70.7 us; the launch traced here: 70.9 us
  starting transfers between devices  33.2 us (47%)
  Pallas kernels  19.1 us (27%)
  waiting for transfers between devices  18.5 us (26%)
    ppermute x17, starting transfers between devices, along(): return lax.ppermute(values, axis, [(i, i ^ step) for i in range(peers)])  21.2 us
    ppermute x17, waiting for transfers between devices, along(): return lax.ppermute(values, axis, [(i, i ^ step) for i in range(peers)])  11.2 us
    ppermute x2, starting transfers between devices, exchange(): other = lax.ppermute(two, 'slab', pairs + [(j, i) for i, j in pairs])  8.32 us
    pallas_call x3, Pallas kernels, mix(): call(functools.partial(mix_kernel, [others[i] for i in members], which, d...  6.85 us
    ppermute x2, waiting for transfers between devices, exchange(): other = lax.ppermute(two, 'slab', pairs + [(j, i) for i, j in pairs])  6.35 us
    pallas_call x1, Pallas kernels, per_device(): call(functools.partial(first_kernel, slabs), [shape_of(3, depth + 2, padd...  4.21 us
    ppermute x1, starting transfers between devices, permute_up(): return lax.ppermute(values, 'slab', [(i, i + 1) for i in range(slabs - 1)])  3.65 us
    pallas_call x1, Pallas kernels, per_device(): call(rims_kernel, [shape_of(7, height, width)] * 2, [SMEM_SPEC, HBM_SPEC,...  3.18 us
  transfers between devices with their start and end apart: 20, of which 10 were waited for; matrix products, arithmetic and copies ran while one was open for 0% of the time, Pallas kernels for 11%

profile of v2, /device:TPU:1, one launch (start us, length us, event | category | flops | bytes accessed | tf_op | source)
XLA Modules:
  0.0 70.9 jit_solution(10198858819230743433)
XLA Ops:
  0.0 0.0 copy-start
  0.0 0.0 copy-start.1
  0.0 0.0 copy-start.2
  0.0 0.0 copy-start.4
  0.0 0.0 copy-start.5
  0.0 3.2 %rims.1 = (f32[7,128,128]{2,1,0:T(8,128)}, f32[7,128,128]{2,1,0:T(8,128)}) custom-call(s32[2,4]{1,0:T(2,128)} %bitcast.10, f32[3,8,128,128]{3,2,1,0:T(8,128)} %bitcast.6, f32[3,8,128,128]{3,2,1,0:T(8,128)} %bitcast.8), custom_call_target="tpu_custom_call" | custom-call | bytes 1835008 | tf_op jit(solution)/shard_map/rims/pallas_call | solution.py:484
  3.2 0.1 collective-permute-start
  3.3 4.6 %collective-permute-start.1 = (f32[7,128,128]{2,1,0:T(8,128)}, f32[7,128,128]{2,1,0:T(8,128)S(1)}, u32[]{:S(2)}, u32[]{:S(2)}) collective-permute-start(f32[7,128,128]{2,1,0:T(8,128)} %get-tuple-element.24), channel_id=1, source_target_pairs={{1,2},{3,4},{5,6},{2,1},{4,3},{6,5},{9,10},{11,12},{13,14},{10,9},... | collective-permute-start | bytes 1376264 | tf_op jit(solution)/shard_map/ppermute | solution.py:428
  7.9 0.0 collective-permute-done.one
  7.9 6.3 %collective-permute-done.1.two = f32[7,128,128]{2,1,0:T(8,128)S(1)} collective-permute-done((f32[7,128,128]{2,1,0:T(8,128)}, f32[7,128,128]{2,1,0:T(8,128)S(1)}, u32[]{:S(2)}, u32[]{:S(2)}) %collective-permute-start.1) | collective-permute-done | bytes 458784 | tf_op jit(solution)/shard_map/ppermute | solution.py:428
  14.2 0.0 copy-done
  14.2 0.0 copy-done.1
  14.2 0.0 copy-done.2
  14.3 0.0 copy-done.4
  14.3 0.0 copy-done.5
  14.3 4.2 %first.1 = (f32[3,10,144,128]{3,2,1,0:T(8,128)S(1)}, f32[3,8,136,128]{3,2,1,0:T(8,128)S(1)}, f32[3,128,128]{2,1,0:T(8,128)S(1)}, f32[3,128,128]{2,1,0:T(8,128)S(...) custom-call(s32[2,4]{1,0:T(2,128)S(1)} %bitcast.11, ...), custom_call_target="tpu_custom_call" | custom-call | flops 78643200 | bytes 9830400 | tf_op jit(solution)/shard_map/first/pallas_call | solution.py:496
  18.5 3.7 %collective-permute-start.2 = (f32[3,128,128]{2,1,0:T(8,128)S(1)}, f32[3,128,128]{2,1,0:T(8,128)S(1)}, u32[]{:S(2)}, u32[]{:S(2)}) collective-permute-start(f32[3,128,128]{2,1,0:T(8,128)S(1)} %get-tuple-element.27), channel_id=1, source_target_pairs={{0,1},{1,2},{2,3},{3,4},{4,5},{5,6},{6,7},{8,9},{9,10},{10,11},{11... | collective-permute-start | bytes 589832 | tf_op jit(solution)/shard_map/ppermute | solution.py:422
  22.2 1.7 %second.1.part = f32[8,128]{1,0:T(8,128)S(1)} custom-call(s32[2,4]{1,0:T(2,128)S(1)} %bitcast.12, f32[3,1,3]{2,1,0:T(1,128)S(1)} %bitcast.20, f32[3,1,3]{2,1,0:T(1,128)S(1)} %bitcast.23, f32[3,8,136,128]{3,2,1,0:T(8,128)S(1)} %get-tuple-element.28.w, f32[8,128,128]{2,1,0:T(8,128)S(1)} %get-tuple-element.29.gx, f32[8,136,128]{2,1,0:T(8,128)S(1)} %get-tuple-element.30.gys, ...), custom_call_target="tpu_custom_call" | custom-call | flops 15728640 | bytes 3276800 | tf_op jit(solution)/shard_map/second/pallas_call | solution.py:520
  23.9 0.9 %collective-permute-done.2.wlo = f32[3,128,128]{2,1,0:T(8,128)S(1)} collective-permute-done((f32[3,128,128]{2,1,0:T(8,128)S(1)}, f32[3,128,128]{2,1,0:T(8,128)S(1)}, u32[]{:S(2)}, u32[]{:S(2)}) %collective-permute-start.2) | collective-permute-done | bytes 196640 | tf_op jit(solution)/shard_map/ppermute | solution.py:422
  24.7 0.6 cross.1
  25.4 0.1 collective-permute-start.3
  25.4 1.2 %collective-permute-done.3 = f32[8,128]{1,0:T(8,128)S(1)} collective-permute-done((f32[8,128]{1,0:T(8,128)S(1)}, f32[8,128]{1,0:T(8,128)S(1)}, u32[]{:S(2)}, u32[]{:S(2)}) %collective-permute-start.3) | collective-permute-done | bytes 4128 | tf_op jit(solution)/shard_map/ppermute | solution.py:434
  26.6 2.3 %collective-permute-start.4 = (f32[8,128]{1,0:T(8,128)S(1)}, f32[8,128]{1,0:T(8,128)S(1)}, u32[]{:S(2)}, u32[]{:S(2)}) collective-permute-start(f32[8,128]{1,0:T(8,128)S(1)} %add.6), channel_id=1, source_target_pairs={{0,2},{1,3},{2,0},{3,1},{4,6},{5,7},{6,4},{7,5},{8,10},{9,11},{10,... | collective-permute-start | bytes 12296 | tf_op jit(solution)/shard_map/ppermute | solution.py:434
  28.9 1.0 %collective-permute-done.4 = f32[8,128]{1,0:T(8,128)S(1)} collective-permute-done((f32[8,128]{1,0:T(8,128)S(1)}, f32[8,128]{1,0:T(8,128)S(1)}, u32[]{:S(2)}, u32[]{:S(2)}) %collective-permute-start.4) | collective-permute-done | bytes 4128 | tf_op jit(solution)/shard_map/ppermute | solution.py:434
  29.9 2.5 %collective-permute-start.5 = (f32[8,128]{1,0:T(8,128)S(1)}, f32[8,128]{1,0:T(8,128)S(1)}, u32[]{:S(2)}, u32[]{:S(2)}) collective-permute-start(f32[8,128]{1,0:T(8,128)S(1)} %add.7.mine), channel_id=1, source_target_pairs={{0,4},{1,5},{2,6},{3,7},{4,0},{5,1},{6,2},{7,3},{8,12},{9,13},{10,... | collective-permute-start | bytes 12296 | tf_op jit(solution)/shard_map/ppermute | solution.py:434
  32.3 1.0 %collective-permute-done.5.theirs = f32[8,128]{1,0:T(8,128)S(1)} collective-permute-done((f32[8,128]{1,0:T(8,128)S(1)}, f32[8,128]{1,0:T(8,128)S(1)}, u32[]{:S(2)}, u32[]{:S(2)}) %collective-permute-start.5) | collective-permute-done | bytes 4128 | tf_op jit(solution)/shard_map/ppermute | solution.py:434
  33.3 0.0 copy-start.3
  33.3 1.2 %solve.1 = (f32[3,8,128,128]{3,2,1,0:T(8,128)S(1)}, f32[3,128,128]{2,1,0:T(8,128)S(1)}, f32[3,128,128]{2,1,0:T(8,128)S(1)}, f32[3,128,128]{2,1,0:T(8,128)S(1)}, f32[3,128,128]{2,1,0:T(8,128)S(1)}) custom-call(s32[2,4]{1,0:T(2,128)S(1)} %bitcast.14, f32[8,128]{1,0:T(8,128)S(1)} %add.7.mine, f32[8,128]{1,0:T(8,128)S(1)} %collective-permute-done.5.theirs, ...), custom_call_target="tpu_custom_call" | custom-call | flops 2097152 | bytes 5898240 | tf_op jit(solution)/shard_map/solve/pallas_call | solution.py:538
  34.5 0.1 collective-permute-start.8
  34.6 1.3 %collective-permute-start.6 = (f32[3,128,128]{2,1,0:T(8,128)S(1)}, f32[3,128,128]{2,1,0:T(8,128)S(1)}, u32[]{:S(2)}, u32[]{:S(2)}) collective-permute-start(f32[3,128,128]{2,1,0:T(8,128)S(1)} %get-tuple-element.35), channel_id=1, source_target_pairs={{0,8},{8,0},{16,24},{24,16},{1,9},{9,1},{17,25},{25,17},{2,10},{10... | collective-permute-start | bytes 589832 | tf_op jit(solution)/shard_map/ppermute | solution.py:434
  35.9 1.4 %collective-permute-start.9 = (f32[3,128,128]{2,1,0:T(8,128)S(1)}, f32[3,128,128]{2,1,0:T(8,128)S(1)}, u32[]{:S(2)}, u32[]{:S(2)}) collective-permute-start(f32[3,128,128]{2,1,0:T(8,128)S(1)} %get-tuple-element.36), channel_id=1, source_target_pairs={{0,16},{8,24},{16,0},{24,8},{1,17},{9,25},{17,1},{25,9},{2,18},{10... | collective-permute-start | bytes 589832 | tf_op jit(solution)/shard_map/ppermute | solution.py:434
  37.2 0.3 collective-permute-start.7
  37.5 1.2 %collective-permute-start.12 = (f32[3,128,128]{2,1,0:T(8,128)S(1)}, f32[3,128,128]{2,1,0:T(8,128)S(1)}, u32[]{:S(2)}, u32[]{:S(2)}) collective-permute-start(f32[3,128,128]{2,1,0:T(8,128)S(1)} %get-tuple-element.37), channel_id=1, source_target_pairs={{0,8},{8,0},{16,24},{24,16},{1,9},{9,1},{17,25},{25,17},{2,10},{10... | collective-permute-start | bytes 589832 | tf_op jit(solution)/shard_map/ppermute | solution.py:434
  38.7 0.4 collective-permute-done.8.refs_2_
  39.1 0.0 collective-permute-start.15
  39.1 0.1 collective-permute-done.6.refs_0_
  39.2 1.7 %collective-permute-start.10 = (f32[3,128,128]{2,1,0:T(8,128)S(1)}, f32[3,128,128]{2,1,0:T(8,128)S(1)}, u32[]{:S(2)}, u32[]{:S(2)}) collective-permute-start(f32[3,128,128]{2,1,0:T(8,128)S(1)} %collective-permute-done.6.refs_0_), channel_id=1, source_target_pairs={{0,16},{8,24},{16,0},{24,8},{1,17},{9,25},{17,1},{25,9},{2,18},{10... | collective-permute-start | bytes 589832 | tf_op jit(solution)/shard_map/ppermute | solution.py:434
  40.8 2.0 %collective-permute-done.9.refs_3_ = f32[3,128,128]{2,1,0:T(8,128)S(1)} collective-permute-done((f32[3,128,128]{2,1,0:T(8,128)S(1)}, f32[3,128,128]{2,1,0:T(8,128)S(1)}, u32[]{:S(2)}, u32[]{:S(2)}) %collective-permute-start.9) | collective-permute-done | bytes 196640 | tf_op jit(solution)/shard_map/ppermute | solution.py:434
  42.9 1.2 %collective-permute-start.11 = (f32[3,128,128]{2,1,0:T(8,128)S(1)}, f32[3,128,128]{2,1,0:T(8,128)S(1)}, u32[]{:S(2)}, u32[]{:S(2)}) collective-permute-start(f32[3,128,128]{2,1,0:T(8,128)S(1)} %collective-permute-done.9.refs_3_), channel_id=1, source_target_pairs={{0,8},{8,0},{16,24},{24,16},{1,9},{9,1},{17,25},{25,17},{2,10},{10... | collective-permute-start | bytes 589832 | tf_op jit(solution)/shard_map/ppermute | solution.py:434
  44.1 0.0 collective-permute-done.7.refs_1_
  44.1 0.3 collective-permute-start.14
  44.4 3.8 %collective-permute-done.12.refs_0_ = f32[3,128,128]{2,1,0:T(8,128)S(1)} collective-permute-done((f32[3,128,128]{2,1,0:T(8,128)S(1)}, f32[3,128,128]{2,1,0:T(8,128)S(1)}, u32[]{:S(2)}, u32[]{:S(2)}) %collective-permute-start.12) | collective-permute-done | bytes 196640 | tf_op jit(solution)/shard_map/ppermute | solution.py:434
  48.2 0.2 collective-permute-start.13
  48.4 0.0 collective-permute-done.15.refs_3_
  48.4 1.1 %collective-permute-start.16 = (f32[3,128,128]{2,1,0:T(8,128)S(1)}, f32[3,128,128]{2,1,0:T(8,128)S(1)}, u32[]{:S(2)}, u32[]{:S(2)}) collective-permute-start(f32[3,128,128]{2,1,0:T(8,128)S(1)} %collective-permute-done.12.refs_0_), channel_id=1, source_target_pairs={{0,16},{8,24},{16,0},{24,8},{1,17},{9,25},{17,1},{25,9},{2,18},{10... | collective-permute-start | bytes 589832 | tf_op jit(solution)/shard_map/ppermute | solution.py:434
  49.5 1.8 %collective-permute-done.10.refs_4_ = f32[3,128,128]{2,1,0:T(8,128)S(1)} collective-permute-done((f32[3,128,128]{2,1,0:T(8,128)S(1)}, f32[3,128,128]{2,1,0:T(8,128)S(1)}, u32[]{:S(2)}, u32[]{:S(2)}) %collective-permute-start.10) | collective-permute-done | bytes 196640 | tf_op jit(solution)/shard_map/ppermute | solution.py:434
  51.3 1.2 %collective-permute-start.17 = (f32[3,128,128]{2,1,0:T(8,128)S(1)}, f32[3,128,128]{2,1,0:T(8,128)S(1)}, u32[]{:S(2)}, u32[]{:S(2)}) collective-permute-start(f32[3,128,128]{2,1,0:T(8,128)S(1)} %collective-permute-done.15.refs_3_), channel_id=1, source_target_pairs={{0,8},{8,0},{16,24},{24,16},{1,9},{9,1},{17,25},{25,17},{2,10},{10... | collective-permute-start | bytes 589832 | tf_op jit(solution)/shard_map/ppermute | solution.py:434
  52.5 0.0 collective-permute-done.11.refs_5_
  52.5 0.0 copy-done.3
  52.5 1.3 %edges.1 = (f32[3,128,128]{2,1,0:T(8,128)S(1)}, f32[3,128,128]{2,1,0:T(8,128)S(1)}) custom-call(s32[2,4]{1,0:T(2,128)S(1)} %bitcast.15, s32[4,3]{1,0:T(4,128)S(1)} %copy-done.3, f32[3,128,128]{2,1,0:T(8,128)S(1)} %collective-permute-done.6.refs_0_, f32[3,128,128]{2,1,0:T(8,128)S(1)} %collective-permute-done.7.refs_1_, ...), custom_call_target="tpu_custom_call" | custom-call | flops 6553600 | bytes 2621440 | tf_op jit(solution)/shard_map/edges/pallas_call | solution.py:550
  53.8 6.4 %collective-permute-start.18 = (f32[3,128,128]{2,1,0:T(8,128)S(1)}, f32[3,128,128]{2,1,0:T(8,128)S(1)}, u32[]{:S(2)}, u32[]{:S(2)}) collective-permute-start(f32[3,128,128]{2,1,0:T(8,128)S(1)} %get-tuple-element.39), channel_id=1, source_target_pairs={{0,1},{1,0},{2,3},{3,2},{4,5},{5,4},{6,7},{7,6},{8,9},{9,8},{10,11... | collective-permute-start | bytes 589832 | tf_op jit(solution)/shard_map/ppermute | solution.py:434
  60.2 0.0 collective-permute-done.14.refs_2_
  60.2 3.7 %collective-permute-start.19 = (f32[3,128,128]{2,1,0:T(8,128)S(1)}, f32[3,128,128]{2,1,0:T(8,128)S(1)}, u32[]{:S(2)}, u32[]{:S(2)}) collective-permute-start(f32[3,128,128]{2,1,0:T(8,128)S(1)} %get-tuple-element.40), channel_id=1, source_target_pairs={{1,2},{3,4},{5,6},{2,1},{4,3},{6,5},{9,10},{11,12},{13,14},{10,9},... | collective-permute-start | bytes 589832 | tf_op jit(solution)/shard_map/ppermute | solution.py:428
  64.0 2.5 %mix_one.1.start = f32[3,8,128,128]{3,2,1,0:T(8,128)S(1)} custom-call(s32[2,4]{1,0:T(2,128)S(1)} %bitcast.16, s32[4,3]{1,0:T(4,128)S(1)} %copy-done.3, f32[3,8,128,128]{3,2,1,0:T(8,128)S(1)} %get-tuple-element.34.start, f32[3,128,128]{2,1,0:T(8,128)S(1)} %collective-permute-done.6.refs_0_, ...), custom_call_target="tpu_custom_call", output_to_operand_aliasing={{}: (2, {})} | custom-call | flops 65536000 | bytes 4325376 | tf_op jit(solution)/shard_map/mix_one/pallas_call | solution.py:564
  66.5 0.0 collective-permute-done.13.refs_1_
  66.5 2.5 %mix_two.1.start = f32[3,8,128,128]{3,2,1,0:T(8,128)S(1)} custom-call(s32[2,4]{1,0:T(2,128)S(1)} %bitcast.17, s32[4,3]{1,0:T(4,128)S(1)} %copy-done.3, f32[3,8,128,128]{3,2,1,0:T(8,128)S(1)} %mix_one.1.start, f32[3,128,128]{2,1,0:T(8,128)S(1)} %collective-permute-done.12.refs_0_, ...), custom_call_target="tpu_custom_call", output_to_operand_aliasing={{}: (2, {})} | custom-call | flops 65536000 | bytes 3932160 | tf_op jit(solution)/shard_map/mix_two/pallas_call | solution.py:564
  68.9 0.0 collective-permute-done.16.refs_0_
  69.0 0.0 collective-permute-done.17.refs_1_
  69.0 0.0 collective-permute-done.18.refs_2_
  69.0 0.0 collective-permute-done.19.refs_3_
  69.0 1.9 %mix_three.1 = f32[3,8,128,128]{3,2,1,0:T(8,128)} custom-call(s32[2,4]{1,0:T(2,128)S(1)} %bitcast.18, s32[4,3]{1,0:T(4,128)S(1)} %copy-done.3, f32[3,8,128,128]{3,2,1,0:T(8,128)S(1)} %mix_two.1.start, f32[3,128,128]{2,1,0:T(8,128)S(1)} %collective-permute-done.16.refs_0_, f32[3,128,128]{2,1,0:T(8,128)S(1)} %collective-permute-done.17.refs_1_, ...), custom_call_target="tpu_custom_call" | custom-call | flops 65536000 | bytes 3932160 | tf_op jit(solution)/shard_map/mix_three/pallas_call | solution.py:564
  (2 shorter events, 0.0 us)
Async XLA Ops:
  0.0 14.2 %copy-start = (f32[1,3,8,128,128]{4,3,2,1,0:T(8,128)S(1)}, f32[1,3,8,128,128]{4,3,2,1,0:T(8,128)}, u32[]{:S(2)}) copy-start(f32[1,3,8,128,128]{4,3,2,1,0:T(8,128)} %param.6) | copy-start | bytes 4718596
  0.0 14.2 %copy-start.1 = (f32[1,3,8,128,128]{4,3,2,1,0:T(8,128)S(1)}, f32[1,3,8,128,128]{4,3,2,1,0:T(8,128)}, u32[]{:S(2)}) copy-start(f32[1,3,8,128,128]{4,3,2,1,0:T(8,128)} %param.7) | copy-start | bytes 4718596
  0.0 14.2 %copy-start.2 = (s32[4,2]{0,1:T(2,128)S(1)}, s32[4,2]{0,1:T(2,128)}, u32[]{:S(2)}) copy-start(s32[4,2]{0,1:T(2,128)} %param.10) | copy-start | bytes 100
  0.0 14.2 %copy-start.4 = (f32[1,3,3]{2,0,1:T(1,128)S(1)}, f32[1,3,3]{2,0,1:T(1,128)}, u32[]{:S(2)}) copy-start(f32[1,3,3]{2,0,1:T(1,128)} %param.8) | copy-start | bytes 112
  0.0 14.2 %copy-start.5 = (f32[1,3,3]{2,0,1:T(1,128)S(1)}, f32[1,3,3]{2,0,1:T(1,128)}, u32[]{:S(2)}) copy-start(f32[1,3,3]{2,0,1:T(1,128)} %param.9) | copy-start | bytes 112
  3.2 4.7 %collective-permute-start = (f32[7,128,128]{2,1,0:T(8,128)}, f32[7,128,128]{2,1,0:T(8,128)S(1)}, u32[]{:S(2)}, u32[]{:S(2)}) collective-permute-start(f32[7,128,128]{2,1,0:T(8,128)} %get-tuple-element.23), channel_id=1, source_target_pairs={{0,1},{1,0},{2,3},{3,2},{4,5},{5,4},{6,7},{7,6},{8,9},{9,8},{10,11... | collective-permute-start | bytes 1376264 | tf_op jit(solution)/shard_map/ppermute | solution.py:434
  3.3 10.9 %collective-permute-start.1 = (f32[7,128,128]{2,1,0:T(8,128)}, f32[7,128,128]{2,1,0:T(8,128)S(1)}, u32[]{:S(2)}, u32[]{:S(2)}) collective-permute-start(f32[7,128,128]{2,1,0:T(8,128)} %get-tuple-element.24), channel_id=1, source_target_pairs={{1,2},{3,4},{5,6},{2,1},{4,3},{6,5},{9,10},{11,12},{13,14},{10,9},... | collective-permute-start | bytes 1376264 | tf_op jit(solution)/shard_map/ppermute | solution.py:428
  18.5 6.3 %collective-permute-start.2 = (f32[3,128,128]{2,1,0:T(8,128)S(1)}, f32[3,128,128]{2,1,0:T(8,128)S(1)}, u32[]{:S(2)}, u32[]{:S(2)}) collective-permute-start(f32[3,128,128]{2,1,0:T(8,128)S(1)} %get-tuple-element.27), channel_id=1, source_target_pairs={{0,1},{1,2},{2,3},{3,4},{4,5},{5,6},{6,7},{8,9},{9,10},{10,11},{11... | collective-permute-start | bytes 589832 | tf_op jit(solution)/shard_map/ppermute | solution.py:422
  25.4 1.2 %collective-permute-start.3 = (f32[8,128]{1,0:T(8,128)S(1)}, f32[8,128]{1,0:T(8,128)S(1)}, u32[]{:S(2)}, u32[]{:S(2)}) collective-permute-start(f32[8,128]{1,0:T(8,128)S(1)} %cross.1), channel_id=1, source_target_pairs={{0,1},{1,0},{2,3},{3,2},{4,5},{5,4},{6,7},{7,6},{8,9},{9,8},{10,11... | collective-permute-start | bytes 12296 | tf_op jit(solution)/shard_map/ppermute | solution.py:434
  26.6 3.2 %collective-permute-start.4 = (f32[8,128]{1,0:T(8,128)S(1)}, f32[8,128]{1,0:T(8,128)S(1)}, u32[]{:S(2)}, u32[]{:S(2)}) collective-permute-start(f32[8,128]{1,0:T(8,128)S(1)} %add.6), channel_id=1, source_target_pairs={{0,2},{1,3},{2,0},{3,1},{4,6},{5,7},{6,4},{7,5},{8,10},{9,11},{10,... | collective-permute-start | bytes 12296 | tf_op jit(solution)/shard_map/ppermute | solution.py:434
  29.9 3.5 %collective-permute-start.5 = (f32[8,128]{1,0:T(8,128)S(1)}, f32[8,128]{1,0:T(8,128)S(1)}, u32[]{:S(2)}, u32[]{:S(2)}) collective-permute-start(f32[8,128]{1,0:T(8,128)S(1)} %add.7.mine), channel_id=1, source_target_pairs={{0,4},{1,5},{2,6},{3,7},{4,0},{5,1},{6,2},{7,3},{8,12},{9,13},{10,... | collective-permute-start | bytes 12296 | tf_op jit(solution)/shard_map/ppermute | solution.py:434
  33.3 19.2 %copy-start.3 = (s32[4,3]{1,0:T(4,128)S(1)}, s32[4,3]{1,0:T(4,128)}, u32[]{:S(2)}) copy-start(s32[4,3]{1,0:T(4,128)} %nb.7) | copy-start | bytes 148
  34.5 4.6 %collective-permute-start.8 = (f32[3,128,128]{2,1,0:T(8,128)S(1)}, f32[3,128,128]{2,1,0:T(8,128)S(1)}, u32[]{:S(2)}, u32[]{:S(2)}) collective-permute-start(f32[3,128,128]{2,1,0:T(8,128)S(1)} %get-tuple-element.35), channel_id=1, source_target_pairs={{0,16},{8,24},{16,0},{24,8},{1,17},{9,25},{17,1},{25,9},{2,18},{10... | collective-permute-start | bytes 589832 | tf_op jit(solution)/shard_map/ppermute | solution.py:434
  34.6 4.6 %collective-permute-start.6 = (f32[3,128,128]{2,1,0:T(8,128)S(1)}, f32[3,128,128]{2,1,0:T(8,128)S(1)}, u32[]{:S(2)}, u32[]{:S(2)}) collective-permute-start(f32[3,128,128]{2,1,0:T(8,128)S(1)} %get-tuple-element.35), channel_id=1, source_target_pairs={{0,8},{8,0},{16,24},{24,16},{1,9},{9,1},{17,25},{25,17},{2,10},{10... | collective-permute-start | bytes 589832 | tf_op jit(solution)/shard_map/ppermute | solution.py:434
  35.9 7.0 %collective-permute-start.9 = (f32[3,128,128]{2,1,0:T(8,128)S(1)}, f32[3,128,128]{2,1,0:T(8,128)S(1)}, u32[]{:S(2)}, u32[]{:S(2)}) collective-permute-start(f32[3,128,128]{2,1,0:T(8,128)S(1)} %get-tuple-element.36), channel_id=1, source_target_pairs={{0,16},{8,24},{16,0},{24,8},{1,17},{9,25},{17,1},{25,9},{2,18},{10... | collective-permute-start | bytes 589832 | tf_op jit(solution)/shard_map/ppermute | solution.py:434
  37.2 6.8 %collective-permute-start.7 = (f32[3,128,128]{2,1,0:T(8,128)S(1)}, f32[3,128,128]{2,1,0:T(8,128)S(1)}, u32[]{:S(2)}, u32[]{:S(2)}) collective-permute-start(f32[3,128,128]{2,1,0:T(8,128)S(1)} %get-tuple-element.36), channel_id=1, source_target_pairs={{0,8},{8,0},{16,24},{24,16},{1,9},{9,1},{17,25},{25,17},{2,10},{10... | collective-permute-start | bytes 589832 | tf_op jit(solution)/shard_map/ppermute | solution.py:434
  37.5 10.7 %collective-permute-start.12 = (f32[3,128,128]{2,1,0:T(8,128)S(1)}, f32[3,128,128]{2,1,0:T(8,128)S(1)}, u32[]{:S(2)}, u32[]{:S(2)}) collective-permute-start(f32[3,128,128]{2,1,0:T(8,128)S(1)} %get-tuple-element.37), channel_id=1, source_target_pairs={{0,8},{8,0},{16,24},{24,16},{1,9},{9,1},{17,25},{25,17},{2,10},{10... | collective-permute-start | bytes 589832 | tf_op jit(solution)/shard_map/ppermute | solution.py:434
  39.1 9.3 %collective-permute-start.15 = (f32[3,128,128]{2,1,0:T(8,128)S(1)}, f32[3,128,128]{2,1,0:T(8,128)S(1)}, u32[]{:S(2)}, u32[]{:S(2)}) collective-permute-start(f32[3,128,128]{2,1,0:T(8,128)S(1)} %get-tuple-element.38), channel_id=1, source_target_pairs={{0,16},{8,24},{16,0},{24,8},{1,17},{9,25},{17,1},{25,9},{2,18},{10... | collective-permute-start | bytes 589832 | tf_op jit(solution)/shard_map/ppermute | solution.py:434
  39.2 12.1 %collective-permute-start.10 = (f32[3,128,128]{2,1,0:T(8,128)S(1)}, f32[3,128,128]{2,1,0:T(8,128)S(1)}, u32[]{:S(2)}, u32[]{:S(2)}) collective-permute-start(f32[3,128,128]{2,1,0:T(8,128)S(1)} %collective-permute-done.6.refs_0_), channel_id=1, source_target_pairs={{0,16},{8,24},{16,0},{24,8},{1,17},{9,25},{17,1},{25,9},{2,18},{10... | collective-permute-start | bytes 589832 | tf_op jit(solution)/shard_map/ppermute | solution.py:434
  42.9 9.6 %collective-permute-start.11 = (f32[3,128,128]{2,1,0:T(8,128)S(1)}, f32[3,128,128]{2,1,0:T(8,128)S(1)}, u32[]{:S(2)}, u32[]{:S(2)}) collective-permute-start(f32[3,128,128]{2,1,0:T(8,128)S(1)} %collective-permute-done.9.refs_3_), channel_id=1, source_target_pairs={{0,8},{8,0},{16,24},{24,16},{1,9},{9,1},{17,25},{25,17},{2,10},{10... | collective-permute-start | bytes 589832 | tf_op jit(solution)/shard_map/ppermute | solution.py:434
  44.1 16.1 %collective-permute-start.14 = (f32[3,128,128]{2,1,0:T(8,128)S(1)}, f32[3,128,128]{2,1,0:T(8,128)S(1)}, u32[]{:S(2)}, u32[]{:S(2)}) collective-permute-start(f32[3,128,128]{2,1,0:T(8,128)S(1)} %get-tuple-element.37), channel_id=1, source_target_pairs={{0,16},{8,24},{16,0},{24,8},{1,17},{9,25},{17,1},{25,9},{2,18},{10... | collective-permute-start | bytes 589832 | tf_op jit(solution)/shard_map/ppermute | solution.py:434
  48.2 18.3 %collective-permute-start.13 = (f32[3,128,128]{2,1,0:T(8,128)S(1)}, f32[3,128,128]{2,1,0:T(8,128)S(1)}, u32[]{:S(2)}, u32[]{:S(2)}) collective-permute-start(f32[3,128,128]{2,1,0:T(8,128)S(1)} %get-tuple-element.38), channel_id=1, source_target_pairs={{0,8},{8,0},{16,24},{24,16},{1,9},{9,1},{17,25},{25,17},{2,10},{10... | collective-permute-start | bytes 589832 | tf_op jit(solution)/shard_map/ppermute | solution.py:434
  48.4 20.6 %collective-permute-start.16 = (f32[3,128,128]{2,1,0:T(8,128)S(1)}, f32[3,128,128]{2,1,0:T(8,128)S(1)}, u32[]{:S(2)}, u32[]{:S(2)}) collective-permute-start(f32[3,128,128]{2,1,0:T(8,128)S(1)} %collective-permute-done.12.refs_0_), channel_id=1, source_target_pairs={{0,16},{8,24},{16,0},{24,8},{1,17},{9,25},{17,1},{25,9},{2,18},{10... | collective-permute-start | bytes 589832 | tf_op jit(solution)/shard_map/ppermute | solution.py:434
  51.3 17.7 %collective-permute-start.17 = (f32[3,128,128]{2,1,0:T(8,128)S(1)}, f32[3,128,128]{2,1,0:T(8,128)S(1)}, u32[]{:S(2)}, u32[]{:S(2)}) collective-permute-start(f32[3,128,128]{2,1,0:T(8,128)S(1)} %collective-permute-done.15.refs_3_), channel_id=1, source_target_pairs={{0,8},{8,0},{16,24},{24,16},{1,9},{9,1},{17,25},{25,17},{2,10},{10... | collective-permute-start | bytes 589832 | tf_op jit(solution)/shard_map/ppermute | solution.py:434
  53.8 15.1 %collective-permute-start.18 = (f32[3,128,128]{2,1,0:T(8,128)S(1)}, f32[3,128,128]{2,1,0:T(8,128)S(1)}, u32[]{:S(2)}, u32[]{:S(2)}) collective-permute-start(f32[3,128,128]{2,1,0:T(8,128)S(1)} %get-tuple-element.39), channel_id=1, source_target_pairs={{0,1},{1,0},{2,3},{3,2},{4,5},{5,4},{6,7},{7,6},{8,9},{9,8},{10,11... | collective-permute-start | bytes 589832 | tf_op jit(solution)/shard_map/ppermute | solution.py:434
  60.2 8.8 %collective-permute-start.19 = (f32[3,128,128]{2,1,0:T(8,128)S(1)}, f32[3,128,128]{2,1,0:T(8,128)S(1)}, u32[]{:S(2)}, u32[]{:S(2)}) collective-permute-start(f32[3,128,128]{2,1,0:T(8,128)S(1)} %get-tuple-element.40), channel_id=1, source_target_pairs={{1,2},{3,4},{5,6},{2,1},{4,3},{6,5},{9,10},{11,12},{13,14},{10,9},... | collective-permute-start | bytes 589832 | tf_op jit(solution)/shard_map/ppermute | solution.py:428

commit v3 on v2

--- a/solution.py
+++ b/solution.py
@@ -47,7 +47,7 @@
     return total
 
 
-def rims_kernel(lev, f_hbm, k_hbm, one, two, sems):
+def rims_kernel(lev, nb, f_hbm, k_hbm, one, two, choice, sems):
     depth = f_hbm.shape[1]
     a = cells(depth, lev[1, lax.axis_index("grp")])
     even = lax.rem(lax.axis_index("slab"), 2) == 0
@@ -65,6 +65,13 @@
             started.append(pltpu.make_async_copy(source, target, sems.at[3 * i + j]))
     for copy in started:
         copy.start()
+    bits = jnp.int32(0)
+    for g in range(nb.shape[0]):
+        for entry in range(3):
+            step = nb[g, entry] ^ g
+            bit = lax.shift_left(jnp.int32(1), jnp.clip(step - 1, 0, 30))
+            bits = bits | jnp.where((nb[g, entry] >= 0) & (step > 0), bit, 0)
+    choice[0] = bits
     for copy in started:
         copy.wait()
 
@@ -443,17 +450,24 @@
     return sums, along(sums, "slab", step)
 
 
-def gather(slots):
-    groups = lax.axis_size("grp")
-    if groups != 4:
-        return [[along(slot, "grp", step) for slot in slots] for step in range(1, groups)]
-    by_x, by_y, by_both = {}, {}, {}
-    for i in range(0, len(slots), 2):
-        j = i + 1
-        by_x[i], by_y[j] = along(slots[i], "grp", 1), along(slots[j], "grp", 2)
-        by_x[j], by_y[i] = along(slots[j], "grp", 1), along(slots[i], "grp", 2)
-        by_both[i], by_both[j] = along(by_x[i], "grp", 2), along(by_y[j], "grp", 1)
-    return [[group[i] for i in range(len(slots))] for group in (by_x, by_y, by_both)]
+def gather(slots, steps):
+    got = {step: {} for step in steps}
+    if 3 not in steps or len(steps) == 1 or max(steps) > 3:
+        for i, slot in enumerate(slots):
+            for step in steps:
+                got[step][i] = along(slot, "grp", step)
+    elif len(steps) == 2:
+        direct = steps[0]
+        for i, slot in enumerate(slots):
+            got[direct][i] = along(slot, "grp", direct)
+            got[3][i] = along(got[direct][i], "grp", 3 ^ direct)
+    else:
+        for i in range(0, len(slots), 2):
+            j = i + 1
+            got[1][i], got[2][j] = along(slots[i], "grp", 1), along(slots[j], "grp", 2)
+            got[1][j], got[2][i] = along(slots[j], "grp", 1), along(slots[i], "grp", 2)
+            got[3][i], got[3][j] = along(got[1][i], "grp", 2), along(got[2][j], "grp", 1)
+    return [[got[step][i] for i in range(len(slots))] for step in steps]
 
 
 def call(kernel, outs, specs_in, specs_out, scratch=(), cost=None, limit=VMEM_LIMIT, **more):
@@ -469,6 +483,57 @@
     )
 
 
+def difference(depth, height, width, steps, levels, neighbours, u, *slots):
+    half = depth // 2
+    plane = 4 * height * width
+    rows3 = shape_of(3, height, width)
+    whole = shape_of(3, depth, height, width)
+    received = gather(slots, steps) if steps else []
+    others = [functools.partial(lambda step, g: g ^ step, step) for step in steps]
+    early = [slot for group in received for slot in group[:2]]
+    if not steps:
+        return call(
+            functools.partial(mix_kernel, [], [], depth, False),
+            whole,
+            [SMEM_SPEC] * 2 + [VMEM_SPEC],
+            VMEM_SPEC,
+            [pltpu.VMEM((width, 2 * width), jnp.bfloat16)],
+            name="mix_none",
+        )(levels, neighbours, u)
+    edge_one, edge_two = call(
+        functools.partial(edges_kernel, others),
+        [rows3] * 2,
+        [SMEM_SPEC] * 2 + [VMEM_SPEC] * len(early),
+        [VMEM_SPEC] * 2,
+        [pltpu.VMEM((width, width), jnp.bfloat16)],
+        estimate(100 * plane, 40 * plane),
+        name="edges",
+    )(levels, neighbours, *early)
+    rims = exchange(edge_one, edge_two)
+
+    def mix(start, members, which, ends, name):
+        pieces = [received[i][j] for i in members for j in which]
+        given = pieces + (list(rims) if ends else [])
+        return call(
+            functools.partial(mix_kernel, [others[i] for i in members], which, depth, ends),
+            whole,
+            [SMEM_SPEC] * 2 + [VMEM_SPEC] * (1 + len(given)),
+            VMEM_SPEC,
+            [pltpu.VMEM((width, 2 * width), jnp.bfloat16)],
+            estimate(1000 * plane, (48 + 3 * len(given)) * plane),
+            input_output_aliases={} if ends else {2: 0},
+            name=name,
+        )(levels, neighbours, start, *given)
+
+    members = list(range(len(received)))
+    mixed = mix(u, members, range(2), False, "mix_one")
+    if len(steps) == 3:
+        mixed = mix(mixed, members[:-1], range(2, half), False, "mix_two")
+        return mix(mixed, members[-1:], range(2, half), True, "mix_three")
+    mixed = mix(mixed, members, range(2, half - 1), False, "mix_two")
+    return mix(mixed, members, range(half - 1, half), True, "mix_three")
+
+
 def per_device(forcing, stiffness, anisotropy, coupling, levels, neighbours):
     _, _, depth, height, width = forcing.shape
     slabs = lax.axis_size("slab")
@@ -481,16 +546,16 @@
     rows3 = shape_of(3, height, width)
     whole = shape_of(3, depth, height, width)
 
-    one, two = call(
+    one, two, choice = call(
         rims_kernel,
-        [shape_of(7, height, width)] * 2,
-        [SMEM_SPEC, HBM_SPEC, HBM_SPEC],
-        [VMEM_SPEC] * 2,
+        [shape_of(7, height, width)] * 2 + [jax.ShapeDtypeStruct((1,), jnp.int32)],
+        [SMEM_SPEC, SMEM_SPEC, HBM_SPEC, HBM_SPEC],
+        [VMEM_SPEC] * 2 + [SMEM_SPEC],
         [pltpu.SemaphoreType.DMA((6,))],
         estimate(0, 28 * plane),
         limit=60 * 1024 * 1024,
         name="rims",
-    )(levels, f, k)
+    )(levels, neighbours, f, k)
     one, two = exchange(one, two)
 
     zs, w, wl, w0, gx, gys, gz, gl, dots = call(
@@ -543,40 +608,15 @@
         cost=estimate(4 * depth * plane, 90 * plane),
         name="solve",
     )(levels, mine, theirs, zs, w)
-    received = gather(slots)
-    steps = range(1, len(received) + 1)
-    others = [functools.partial(lambda step, g: g ^ step, step) for step in steps]
-    early = [slot for group in received for slot in group[:2]]
-    edge_one, edge_two = call(
-        functools.partial(edges_kernel, others),
-        [rows3] * 2,
-        [SMEM_SPEC] * 2 + [VMEM_SPEC] * len(early),
-        [VMEM_SPEC] * 2,
-        [pltpu.VMEM((width, width), jnp.bfloat16)],
-        estimate(100 * plane, 40 * plane),
-        name="edges",
-    )(levels, neighbours, *early)
-    rims = exchange(edge_one, edge_two)
-
-    def mix(start, members, which, ends, name):
-        pieces = [received[i][j] for i in members for j in which]
-        given = pieces + (list(rims) if ends else [])
-        return call(
-            functools.partial(mix_kernel, [others[i] for i in members], which, depth, ends),
-            whole,
-            [SMEM_SPEC] * 2 + [VMEM_SPEC] * (1 + len(given)),
-            VMEM_SPEC,
-            [pltpu.VMEM((width, 2 * width), jnp.bfloat16)],
-            estimate(1000 * plane, (48 + 3 * len(given)) * plane),
-            input_output_aliases={} if ends else {2: 0},
-            name=name,
-        )(levels, neighbours, start, *given)
-
-    members = list(range(len(received)))
-    mixed = mix(u, members, range(2), False, "mix_one")
-    mixed = mix(mixed, members[:-1], range(2, half), False, "mix_two")
-    mixed = mix(mixed, members[-1:], range(2, half), True, "mix_three")
-    return mixed[None]
+    combine = functools.partial(difference, depth, height, width)
+    groups = lax.axis_size("grp")
+    if groups != 4:
+        return combine(tuple(range(1, groups)), levels, neighbours, u, *slots)[None]
+    branches = [
+        functools.partial(combine, tuple(s for i, s in enumerate((1, 2, 3)) if mask >> i & 1))
+        for mask in range(8)
+    ]
+    return lax.switch(choice[0], branches, levels, neighbours, u, *slots)[None]
 
 
 def solution(mesh):

time: 70.7 us -> 67.8 us (0.959)
  the two profiles are of different devices: /device:TPU:1 before, /device:TPU:19 now
where the time goes in v3:
time: 67.8 us; the launch traced here: 67.6 us
  waiting for transfers between devices  25.4 us (37%)
  starting transfers between devices  21 us (31%)
  Pallas kernels  18.8 us (28%)
  local copies, waits for them, and re-layouts  1.16 us (2%)
  between operations  0.74 us (1%)
    ppermute x13, waiting for transfers between devices, along(): return lax.ppermute(values, axis, [(i, i ^ step) for i in range(peers)])  17.6 us
    ppermute x13, starting transfers between devices, along(): return lax.ppermute(values, axis, [(i, i ^ step) for i in range(peers)])  11.7 us
    ppermute x2, waiting for transfers between devices, exchange(): other = lax.ppermute(two, 'slab', pairs + [(j, i) for i, j in pairs])  6.88 us
    pallas_call x3, Pallas kernels, mix(): call(functools.partial(mix_kernel, [others[i] for i in members], which, d...  6.63 us
    ppermute x2, starting transfers between devices, exchange(): other = lax.ppermute(two, 'slab', pairs + [(j, i) for i, j in pairs])  6.21 us
    pallas_call x1, Pallas kernels, per_device(): call(functools.partial(first_kernel, slabs), [shape_of(3, depth + 2, padd...  4.21 us
    pallas_call x1, Pallas kernels, per_device(): call(rims_kernel, [shape_of(7, height, width)] * 2 + [jax.ShapeDtypeStruc...  3.19 us
    ppermute x1, starting transfers between devices, permute_up(): return lax.ppermute(values, 'slab', [(i, i + 1) for i in range(slabs - 1)])  3.12 us
  transfers between devices with their start and end apart: 16, of which 9 were waited for; matrix products, arithmetic and copies ran while one was open for 0% of the time, Pallas kernels for 11%

profile of v3, /device:TPU:19, one launch (start us, length us, event | category | flops | bytes accessed | tf_op | source)
XLA Modules:
  0.0 67.6 jit_solution(772411315438633305)
XLA Ops:
  0.0 0.0 copy-start
  0.0 0.0 copy-start.1
  0.0 0.0 copy-start.2
  0.0 0.0 copy-start.3
  0.0 0.0 copy-start.6
  0.0 3.2 %rims.1 = (f32[7,128,128]{2,1,0:T(8,128)}, f32[7,128,128]{2,1,0:T(8,128)}, s32[1]{0:T(128)}) custom-call(s32[2,4]{1,0:T(2,128)} %bitcast.31, s32[4,3]{1,0:T(4,128)} %nb.1, f32[3,8,128,128]{3,2,1,0:T(8,128)} %bitcast.14, f32[3,8,128,128]{3,2,1,0:T(8,128)} %bitcast.16), custom_call_target="tpu_custom_call" | custom-call | bytes 1835008 | tf_op jit(solution)/shard_map/rims/pallas_call | solution.py:549
  3.2 0.7 %collective-permute-start.62 = (f32[7,128,128]{2,1,0:T(8,128)}, f32[7,128,128]{2,1,0:T(8,128)S(1)}, u32[]{:S(2)}, u32[]{:S(2)}) collective-permute-start(f32[7,128,128]{2,1,0:T(8,128)} %get-tuple-element.203), channel_id=1, source_target_pairs={{0,1},{1,0},{2,3},{3,2},{4,5},{5,4},{6,7},{7,6},{8,9},{9,8},{10,11... | collective-permute-start | bytes 1376264 | tf_op jit(solution)/shard_map/ppermute | solution.py:441
  4.0 3.1 %collective-permute-start.63 = (f32[7,128,128]{2,1,0:T(8,128)}, f32[7,128,128]{2,1,0:T(8,128)S(1)}, u32[]{:S(2)}, u32[]{:S(2)}) collective-permute-start(f32[7,128,128]{2,1,0:T(8,128)} %get-tuple-element.204), channel_id=1, source_target_pairs={{1,2},{3,4},{5,6},{2,1},{4,3},{6,5},{9,10},{11,12},{13,14},{10,9},... | collective-permute-start | bytes 1376264 | tf_op jit(solution)/shard_map/ppermute | solution.py:435
  7.1 0.0 collective-permute-done.62.one
  7.1 6.9 %collective-permute-done.63.two = f32[7,128,128]{2,1,0:T(8,128)S(1)} collective-permute-done((f32[7,128,128]{2,1,0:T(8,128)}, f32[7,128,128]{2,1,0:T(8,128)S(1)}, u32[]{:S(2)}, u32[]{:S(2)}) %collective-permute-start.63) | collective-permute-done | bytes 458784 | tf_op jit(solution)/shard_map/ppermute | solution.py:435
  14.0 0.0 copy-done
  14.0 0.0 copy-done.1
  14.0 0.0 copy-done.2
  14.0 0.0 copy-done.3
  14.0 0.0 copy-done.6
  14.0 4.2 %first.1 = (f32[3,10,144,128]{3,2,1,0:T(8,128)S(1)}, f32[3,8,136,128]{3,2,1,0:T(8,128)S(1)}, f32[3,128,128]{2,1,0:T(8,128)S(1)}, f32[3,128,128]{2,1,0:T(8,128)S(...) custom-call(s32[2,4]{1,0:T(2,128)S(1)} %bitcast.32, ...), custom_call_target="tpu_custom_call" | custom-call | flops 78643200 | bytes 9830400 | tf_op jit(solution)/shard_map/first/pallas_call | solution.py:561
  18.2 3.1 %collective-permute-start.64 = (f32[3,128,128]{2,1,0:T(8,128)S(1)}, f32[3,128,128]{2,1,0:T(8,128)S(1)}, u32[]{:S(2)}, u32[]{:S(2)}) collective-permute-start(f32[3,128,128]{2,1,0:T(8,128)S(1)} %get-tuple-element.207), channel_id=1, source_target_pairs={{0,1},{1,2},{2,3},{3,4},{4,5},{5,6},{6,7},{8,9},{9,10},{10,11},{11... | collective-permute-start | bytes 589832 | tf_op jit(solution)/shard_map/ppermute | solution.py:429
  21.3 1.7 %second.1.part = f32[8,128]{1,0:T(8,128)S(1)} custom-call(s32[2,4]{1,0:T(2,128)S(1)} %bitcast.33, f32[3,1,3]{2,1,0:T(1,128)S(1)} %bitcast.19, f32[3,1,3]{2,1,0:T(1,128)S(1)} %bitcast.22, f32[3,8,136,128]{3,2,1,0:T(8,128)S(1)} %get-tuple-element.208.w, f32[8,128,128]{2,1,0:T(8,128)S(1)} %get-tuple-element.209.gx, f32[8,136,128]{2,1,0:T(8,128)S(1)} %get-tuple-element.210.gys, ...), custom_call_target="tpu_custom_call" | custom-call | flops 15728640 | bytes 3276800 | tf_op jit(solution)/shard_map/second/pallas_call | solution.py:585
  23.0 0.9 %collective-permute-done.64.wlo = f32[3,128,128]{2,1,0:T(8,128)S(1)} collective-permute-done((f32[3,128,128]{2,1,0:T(8,128)S(1)}, f32[3,128,128]{2,1,0:T(8,128)S(1)}, u32[]{:S(2)}, u32[]{:S(2)}) %collective-permute-start.64) | collective-permute-done | bytes 196640 | tf_op jit(solution)/shard_map/ppermute | solution.py:429
  23.9 0.6 cross.1
  24.5 1.4 %collective-permute-start.65 = (f32[8,128]{1,0:T(8,128)S(1)}, f32[8,128]{1,0:T(8,128)S(1)}, u32[]{:S(2)}, u32[]{:S(2)}) collective-permute-start(f32[8,128]{1,0:T(8,128)S(1)} %cross.1), channel_id=1, source_target_pairs={{0,1},{1,0},{2,3},{3,2},{4,5},{5,4},{6,7},{7,6},{8,9},{9,8},{10,11... | collective-permute-start | bytes 12296 | tf_op jit(solution)/shard_map/ppermute | solution.py:441
  25.9 0.8 %collective-permute-done.65 = f32[8,128]{1,0:T(8,128)S(1)} collective-permute-done((f32[8,128]{1,0:T(8,128)S(1)}, f32[8,128]{1,0:T(8,128)S(1)}, u32[]{:S(2)}, u32[]{:S(2)}) %collective-permute-start.65) | collective-permute-done | bytes 4128 | tf_op jit(solution)/shard_map/ppermute | solution.py:441
  26.7 1.3 %collective-permute-start.66 = (f32[8,128]{1,0:T(8,128)S(1)}, f32[8,128]{1,0:T(8,128)S(1)}, u32[]{:S(2)}, u32[]{:S(2)}) collective-permute-start(f32[8,128]{1,0:T(8,128)S(1)} %add.6), channel_id=1, source_target_pairs={{0,2},{1,3},{2,0},{3,1},{4,6},{5,7},{6,4},{7,5},{8,10},{9,11},{10,... | collective-permute-start | bytes 12296 | tf_op jit(solution)/shard_map/ppermute | solution.py:441
  28.0 1.2 %collective-permute-done.66 = f32[8,128]{1,0:T(8,128)S(1)} collective-permute-done((f32[8,128]{1,0:T(8,128)S(1)}, f32[8,128]{1,0:T(8,128)S(1)}, u32[]{:S(2)}, u32[]{:S(2)}) %collective-permute-start.66) | collective-permute-done | bytes 4128 | tf_op jit(solution)/shard_map/ppermute | solution.py:441
  29.2 0.0 collective-permute-start.67
  29.8 2.7 %collective-permute-done.67.theirs = f32[8,128]{1,0:T(8,128)S(1)} collective-permute-done((f32[8,128]{1,0:T(8,128)S(1)}, f32[8,128]{1,0:T(8,128)S(1)}, u32[]{:S(2)}, u32[]{:S(2)}) %collective-permute-start.67) | collective-permute-done | bytes 4128 | tf_op jit(solution)/shard_map/ppermute | solution.py:441
  32.6 0.0 copy-start.4
  32.6 1.2 %solve.1 = (f32[3,8,128,128]{3,2,1,0:T(8,128)S(1)}, f32[3,128,128]{2,1,0:T(8,128)S(1)}, f32[3,128,128]{2,1,0:T(8,128)S(1)}, f32[3,128,128]{2,1,0:T(8,128)S(1)}, f32[3,128,128]{2,1,0:T(8,128)S(1)}) custom-call(s32[2,4]{1,0:T(2,128)S(1)} %bitcast.35, f32[8,128]{1,0:T(8,128)S(1)} %add.7.mine, f32[8,128]{1,0:T(8,128)S(1)} %collective-permute-done.67.theirs, ...), custom_call_target="tpu_custom_call" | custom-call | flops 2097152 | bytes 5898240 | tf_op jit(solution)/shard_map/solve/pallas_call | solution.py:603
  33.7 0.0 copy-done.4
  33.7 32.7 %conditional.1 = (f32[1,3,8,128,128]{4,3,2,1,0:T(8,128)S(1)}) conditional(s32[]{:T(128)} %bitcast.11, (s32[2,4]{1,0:T(2,128)S(1)}, s32[4,3]{1,0:T(4,128)S(1)}, f32[3,8,128,128]{3,2,1,0:T(8,128)S(1)}) %tuple.64, (f32[3,128,128]{2,1,0:T(8,128)S(1)}, f32[3,128,128]{2,1,0:T(8,128)S(1)}, s32[2,4]{1,0:T(2,128)S(1)}, ...), branch_computations={%region_0.0_spmd, %region_1.0_spmd, %region_2.0_spmd, %region_3.0_... | conditional | flops 203161600 | bytes 25821752 | solution.py:619
  34.0 0.1 collective-permute-start.38
  34.0 1.5 %collective-permute-start.39 = (f32[3,128,128]{2,1,0:T(8,128)S(1)}, f32[3,128,128]{2,1,0:T(8,128)S(1)}, u32[]{:S(2)}, u32[]{:S(2)}) collective-permute-start(f32[3,128,128]{2,1,0:T(8,128)S(1)} %get-tuple-element.171), channel_id=1, source_target_pairs={{0,16},{8,24},{16,0},{24,8},{1,17},{9,25},{17,1},{25,9},{2,18},{10... | collective-permute-start | bytes 589832 | tf_op jit(solution)/shard_map/cond/branch_6_fun/ppermute | solution.py:441
  35.5 0.1 collective-permute-start.42
  35.6 1.4 %collective-permute-start.44 = (f32[3,128,128]{2,1,0:T(8,128)S(1)}, f32[3,128,128]{2,1,0:T(8,128)S(1)}, u32[]{:S(2)}, u32[]{:S(2)}) collective-permute-start(f32[3,128,128]{2,1,0:T(8,128)S(1)} %get-tuple-element.173), channel_id=1, source_target_pairs={{0,16},{8,24},{16,0},{24,8},{1,17},{9,25},{17,1},{25,9},{2,18},{10... | collective-permute-start | bytes 589832 | tf_op jit(solution)/shard_map/cond/branch_6_fun/ppermute | solution.py:441
  37.0 1.6 %collective-permute-done.38.refs_0_ = f32[3,128,128]{2,1,0:T(8,128)S(1)} collective-permute-done((f32[3,128,128]{2,1,0:T(8,128)S(1)}, f32[3,128,128]{2,1,0:T(8,128)S(1)}, u32[]{:S(2)}, u32[]{:S(2)}) %collective-permute-start.38) | collective-permute-done | bytes 196640 | tf_op jit(solution)/shard_map/cond/branch_6_fun/ppermute | solution.py:441
  38.5 0.0 collective-permute-start.40
  38.6 3.5 %collective-permute-done.39.refs_1_ = f32[3,128,128]{2,1,0:T(8,128)S(1)} collective-permute-done((f32[3,128,128]{2,1,0:T(8,128)S(1)}, f32[3,128,128]{2,1,0:T(8,128)S(1)}, u32[]{:S(2)}, u32[]{:S(2)}) %collective-permute-start.39) | collective-permute-done | bytes 196640 | tf_op jit(solution)/shard_map/cond/branch_6_fun/ppermute | solution.py:441
  42.1 0.3 collective-permute-start.41
  42.4 3.9 %collective-permute-done.42.refs_0_ = f32[3,128,128]{2,1,0:T(8,128)S(1)} collective-permute-done((f32[3,128,128]{2,1,0:T(8,128)S(1)}, f32[3,128,128]{2,1,0:T(8,128)S(1)}, u32[]{:S(2)}, u32[]{:S(2)}) %collective-permute-start.42) | collective-permute-done | bytes 196640 | tf_op jit(solution)/shard_map/cond/branch_6_fun/ppermute | solution.py:441
  46.3 0.3 collective-permute-start.43
  46.6 3.9 %collective-permute-done.44.refs_0_ = f32[3,128,128]{2,1,0:T(8,128)S(1)} collective-permute-done((f32[3,128,128]{2,1,0:T(8,128)S(1)}, f32[3,128,128]{2,1,0:T(8,128)S(1)}, u32[]{:S(2)}, u32[]{:S(2)}) %collective-permute-start.44) | collective-permute-done | bytes 196640 | tf_op jit(solution)/shard_map/cond/branch_6_fun/ppermute | solution.py:441
  50.5 0.3 collective-permute-start.45
  50.8 0.0 collective-permute-done.40.refs_2_
  50.8 0.0 collective-permute-done.41.refs_3_
  50.8 1.3 %edges.12 = (f32[3,128,128]{2,1,0:T(8,128)S(1)}, f32[3,128,128]{2,1,0:T(8,128)S(1)}) custom-call(s32[2,4]{1,0:T(2,128)S(1)} %get-tuple-element.167.lev, s32[4,3]{1,0:T(4,128)S(1)} %get-tuple-element.168.nb, f32[3,128,128]{2,1,0:T(8,128)S(1)} %collective-permute-done.38.refs_0_, f32[3,128,128]{2,1,0:T(8,128)S(1)} %collective-permute-done.39.refs_1_, ...), custom_call_target="tpu_custom_call" | custom-call | flops 6553600 | bytes 2621440 | tf_op jit(solution)/shard_map/cond/branch_6_fun/edges/pallas_call | solution.py:503
  52.1 4.3 %collective-permute-start.46 = (f32[3,128,128]{2,1,0:T(8,128)S(1)}, f32[3,128,128]{2,1,0:T(8,128)S(1)}, u32[]{:S(2)}, u32[]{:S(2)}) collective-permute-start(f32[3,128,128]{2,1,0:T(8,128)S(1)} %get-tuple-element.174), channel_id=1, source_target_pairs={{0,1},{1,0},{2,3},{3,2},{4,5},{5,4},{6,7},{7,6},{8,9},{9,8},{10,11... | collective-permute-start | bytes 589832 | tf_op jit(solution)/shard_map/cond/branch_6_fun/ppermute | solution.py:441
  56.4 3.1 %collective-permute-start.47 = (f32[3,128,128]{2,1,0:T(8,128)S(1)}, f32[3,128,128]{2,1,0:T(8,128)S(1)}, u32[]{:S(2)}, u32[]{:S(2)}) collective-permute-start(f32[3,128,128]{2,1,0:T(8,128)S(1)} %get-tuple-element.175), channel_id=1, source_target_pairs={{1,2},{3,4},{5,6},{2,1},{4,3},{6,5},{9,10},{11,12},{13,14},{10,9},... | collective-permute-start | bytes 589832 | tf_op jit(solution)/shard_map/cond/branch_6_fun/ppermute | solution.py:435
  59.5 2.4 %mix_one.12.start = f32[3,8,128,128]{3,2,1,0:T(8,128)S(1)} custom-call(s32[2,4]{1,0:T(2,128)S(1)} %get-tuple-element.167.lev, s32[4,3]{1,0:T(4,128)S(1)} %get-tuple-element.168.nb, f32[3,8,128,128]{3,2,1,0:T(8,128)S(1)} %get-tuple-element.169.start, f32[3,128,128]{2,1,0:T(8,128)S(1)} %collective-permute-done.38.refs_0_, ...), custom_call_target="tpu_custom_call", output_to_operand_aliasing={{}: (2, {})} | custom-call | flops 65536000 | bytes 3932160 | tf_op jit(solution)/shard_map/cond/branch_6_fun/mix_one/pallas_call | solution.py:517
  62.0 0.0 collective-permute-done.43.refs_1_
  62.0 2.1 %mix_two.12.start = f32[3,8,128,128]{3,2,1,0:T(8,128)S(1)} custom-call(s32[2,4]{1,0:T(2,128)S(1)} %get-tuple-element.167.lev, s32[4,3]{1,0:T(4,128)S(1)} %get-tuple-element.168.nb, f32[3,8,128,128]{3,2,1,0:T(8,128)S(1)} %mix_one.12.start, f32[3,128,128]{2,1,0:T(8,128)S(1)} %collective-permute-done.42.refs_0_, ...), custom_call_target="tpu_custom_call", output_to_operand_aliasing={{}: (2, {})} | custom-call | flops 65536000 | bytes 3538944 | tf_op jit(solution)/shard_map/cond/branch_6_fun/mix_two/pallas_call | solution.py:517
  64.1 0.0 collective-permute-done.45.refs_1_
  64.1 0.0 collective-permute-done.46.refs_2_
  64.1 0.0 collective-permute-done.47.refs_3_
  64.1 2.1 %mix_three.12 = f32[3,8,128,128]{3,2,1,0:T(8,128)S(1)} custom-call(s32[2,4]{1,0:T(2,128)S(1)} %get-tuple-element.167.lev, s32[4,3]{1,0:T(4,128)S(1)} %get-tuple-element.168.nb, f32[3,8,128,128]{3,2,1,0:T(8,128)S(1)} %mix_two.12.start, f32[3,128,128]{2,1,0:T(8,128)S(1)} %collective-permute-done.44.refs_0_, ...), custom_call_target="tpu_custom_call" | custom-call | flops 65536000 | bytes 3932160 | tf_op jit(solution)/shard_map/cond/branch_6_fun/mix_three/pallas_call | solution.py:517
  66.5 0.0 copy-start.5
  66.5 1.1 %copy-done.5 = f32[1,3,8,128,128]{4,3,2,1,0:T(8,128)} copy-done((f32[1,3,8,128,128]{4,3,2,1,0:T(8,128)}, f32[1,3,8,128,128]{4,3,2,1,0:T(8,128)S(1)}, u32[]{:S(2)}) %copy-start.5) | copy-done | bytes 1572888
  (2 shorter events, 0.0 us)
Async XLA Ops:
  0.0 14.0 %copy-start = (f32[1,3,8,128,128]{4,3,2,1,0:T(8,128)S(1)}, f32[1,3,8,128,128]{4,3,2,1,0:T(8,128)}, u32[]{:S(2)}) copy-start(f32[1,3,8,128,128]{4,3,2,1,0:T(8,128)} %param.14) | copy-start | bytes 4718596
  0.0 14.0 %copy-start.1 = (f32[1,3,8,128,128]{4,3,2,1,0:T(8,128)S(1)}, f32[1,3,8,128,128]{4,3,2,1,0:T(8,128)}, u32[]{:S(2)}) copy-start(f32[1,3,8,128,128]{4,3,2,1,0:T(8,128)} %param.15) | copy-start | bytes 4718596
  0.0 14.0 %copy-start.2 = (f32[1,3,3]{2,0,1:T(1,128)S(1)}, f32[1,3,3]{2,0,1:T(1,128)}, u32[]{:S(2)}) copy-start(f32[1,3,3]{2,0,1:T(1,128)} %param.16) | copy-start | bytes 112
  0.0 14.0 %copy-start.3 = (f32[1,3,3]{2,0,1:T(1,128)S(1)}, f32[1,3,3]{2,0,1:T(1,128)}, u32[]{:S(2)}) copy-start(f32[1,3,3]{2,0,1:T(1,128)} %param.17) | copy-start | bytes 112
  0.0 14.0 %copy-start.6 = (s32[4,2]{0,1:T(2,128)S(1)}, s32[4,2]{0,1:T(2,128)}, u32[]{:S(2)}) copy-start(s32[4,2]{0,1:T(2,128)} %param.18) | copy-start | bytes 100
  3.2 3.9 %collective-permute-start.62 = (f32[7,128,128]{2,1,0:T(8,128)}, f32[7,128,128]{2,1,0:T(8,128)S(1)}, u32[]{:S(2)}, u32[]{:S(2)}) collective-permute-start(f32[7,128,128]{2,1,0:T(8,128)} %get-tuple-element.203), channel_id=1, source_target_pairs={{0,1},{1,0},{2,3},{3,2},{4,5},{5,4},{6,7},{7,6},{8,9},{9,8},{10,11... | collective-permute-start | bytes 1376264 | tf_op jit(solution)/shard_map/ppermute | solution.py:441
  4.0 10.0 %collective-permute-start.63 = (f32[7,128,128]{2,1,0:T(8,128)}, f32[7,128,128]{2,1,0:T(8,128)S(1)}, u32[]{:S(2)}, u32[]{:S(2)}) collective-permute-start(f32[7,128,128]{2,1,0:T(8,128)} %get-tuple-element.204), channel_id=1, source_target_pairs={{1,2},{3,4},{5,6},{2,1},{4,3},{6,5},{9,10},{11,12},{13,14},{10,9},... | collective-permute-start | bytes 1376264 | tf_op jit(solution)/shard_map/ppermute | solution.py:435
  18.2 5.7 %collective-permute-start.64 = (f32[3,128,128]{2,1,0:T(8,128)S(1)}, f32[3,128,128]{2,1,0:T(8,128)S(1)}, u32[]{:S(2)}, u32[]{:S(2)}) collective-permute-start(f32[3,128,128]{2,1,0:T(8,128)S(1)} %get-tuple-element.207), channel_id=1, source_target_pairs={{0,1},{1,2},{2,3},{3,4},{4,5},{5,6},{6,7},{8,9},{9,10},{10,11},{11... | collective-permute-start | bytes 589832 | tf_op jit(solution)/shard_map/ppermute | solution.py:429
  24.5 2.2 %collective-permute-start.65 = (f32[8,128]{1,0:T(8,128)S(1)}, f32[8,128]{1,0:T(8,128)S(1)}, u32[]{:S(2)}, u32[]{:S(2)}) collective-permute-start(f32[8,128]{1,0:T(8,128)S(1)} %cross.1), channel_id=1, source_target_pairs={{0,1},{1,0},{2,3},{3,2},{4,5},{5,4},{6,7},{7,6},{8,9},{9,8},{10,11... | collective-permute-start | bytes 12296 | tf_op jit(solution)/shard_map/ppermute | solution.py:441
  26.7 2.5 %collective-permute-start.66 = (f32[8,128]{1,0:T(8,128)S(1)}, f32[8,128]{1,0:T(8,128)S(1)}, u32[]{:S(2)}, u32[]{:S(2)}) collective-permute-start(f32[8,128]{1,0:T(8,128)S(1)} %add.6), channel_id=1, source_target_pairs={{0,2},{1,3},{2,0},{3,1},{4,6},{5,7},{6,4},{7,5},{8,10},{9,11},{10,... | collective-permute-start | bytes 12296 | tf_op jit(solution)/shard_map/ppermute | solution.py:441
  29.2 3.4 %collective-permute-start.67 = (f32[8,128]{1,0:T(8,128)S(1)}, f32[8,128]{1,0:T(8,128)S(1)}, u32[]{:S(2)}, u32[]{:S(2)}) collective-permute-start(f32[8,128]{1,0:T(8,128)S(1)} %add.7.mine), channel_id=1, source_target_pairs={{0,4},{1,5},{2,6},{3,7},{4,0},{5,1},{6,2},{7,3},{8,12},{9,13},{10,... | collective-permute-start | bytes 12296 | tf_op jit(solution)/shard_map/ppermute | solution.py:441
  32.6 1.2 %copy-start.4 = (s32[4,3]{1,0:T(4,128)S(1)}, s32[4,3]{1,0:T(4,128)}, u32[]{:S(2)}) copy-start(s32[4,3]{1,0:T(4,128)} %nb.1) | copy-start | bytes 148
  34.0 4.6 %collective-permute-start.38 = (f32[3,128,128]{2,1,0:T(8,128)S(1)}, f32[3,128,128]{2,1,0:T(8,128)S(1)}, u32[]{:S(2)}, u32[]{:S(2)}) collective-permute-start(f32[3,128,128]{2,1,0:T(8,128)S(1)} %get-tuple-element.170), channel_id=1, source_target_pairs={{0,16},{8,24},{16,0},{24,8},{1,17},{9,25},{17,1},{25,9},{2,18},{10... | collective-permute-start | bytes 589832 | tf_op jit(solution)/shard_map/cond/branch_6_fun/ppermute | solution.py:441
  34.0 8.0 %collective-permute-start.39 = (f32[3,128,128]{2,1,0:T(8,128)S(1)}, f32[3,128,128]{2,1,0:T(8,128)S(1)}, u32[]{:S(2)}, u32[]{:S(2)}) collective-permute-start(f32[3,128,128]{2,1,0:T(8,128)S(1)} %get-tuple-element.171), channel_id=1, source_target_pairs={{0,16},{8,24},{16,0},{24,8},{1,17},{9,25},{17,1},{25,9},{2,18},{10... | collective-permute-start | bytes 589832 | tf_op jit(solution)/shard_map/cond/branch_6_fun/ppermute | solution.py:441
  35.5 10.8 %collective-permute-start.42 = (f32[3,128,128]{2,1,0:T(8,128)S(1)}, f32[3,128,128]{2,1,0:T(8,128)S(1)}, u32[]{:S(2)}, u32[]{:S(2)}) collective-permute-start(f32[3,128,128]{2,1,0:T(8,128)S(1)} %get-tuple-element.172), channel_id=1, source_target_pairs={{0,16},{8,24},{16,0},{24,8},{1,17},{9,25},{17,1},{25,9},{2,18},{10... | collective-permute-start | bytes 589832 | tf_op jit(solution)/shard_map/cond/branch_6_fun/ppermute | solution.py:441
  35.6 14.9 %collective-permute-start.44 = (f32[3,128,128]{2,1,0:T(8,128)S(1)}, f32[3,128,128]{2,1,0:T(8,128)S(1)}, u32[]{:S(2)}, u32[]{:S(2)}) collective-permute-start(f32[3,128,128]{2,1,0:T(8,128)S(1)} %get-tuple-element.173), channel_id=1, source_target_pairs={{0,16},{8,24},{16,0},{24,8},{1,17},{9,25},{17,1},{25,9},{2,18},{10... | collective-permute-start | bytes 589832 | tf_op jit(solution)/shard_map/cond/branch_6_fun/ppermute | solution.py:441
  38.5 12.3 %collective-permute-start.40 = (f32[3,128,128]{2,1,0:T(8,128)S(1)}, f32[3,128,128]{2,1,0:T(8,128)S(1)}, u32[]{:S(2)}, u32[]{:S(2)}) collective-permute-start(f32[3,128,128]{2,1,0:T(8,128)S(1)} %collective-permute-done.38.refs_0_), channel_id=1, source_target_pairs={{0,8},{8,0},{16,24},{24,16},{1,9},{9,1},{17,25},{25,17},{2,10},{10... | collective-permute-start | bytes 589832 | tf_op jit(solution)/shard_map/cond/branch_6_fun/ppermute | solution.py:441
  42.1 8.7 %collective-permute-start.41 = (f32[3,128,128]{2,1,0:T(8,128)S(1)}, f32[3,128,128]{2,1,0:T(8,128)S(1)}, u32[]{:S(2)}, u32[]{:S(2)}) collective-permute-start(f32[3,128,128]{2,1,0:T(8,128)S(1)} %collective-permute-done.39.refs_1_), channel_id=1, source_target_pairs={{0,8},{8,0},{16,24},{24,16},{1,9},{9,1},{17,25},{25,17},{2,10},{10... | collective-permute-start | bytes 589832 | tf_op jit(solution)/shard_map/cond/branch_6_fun/ppermute | solution.py:441
  46.3 15.7 %collective-permute-start.43 = (f32[3,128,128]{2,1,0:T(8,128)S(1)}, f32[3,128,128]{2,1,0:T(8,128)S(1)}, u32[]{:S(2)}, u32[]{:S(2)}) collective-permute-start(f32[3,128,128]{2,1,0:T(8,128)S(1)} %collective-permute-done.42.refs_0_), channel_id=1, source_target_pairs={{0,8},{8,0},{16,24},{24,16},{1,9},{9,1},{17,25},{25,17},{2,10},{10... | collective-permute-start | bytes 589832 | tf_op jit(solution)/shard_map/cond/branch_6_fun/ppermute | solution.py:441
  50.5 13.6 %collective-permute-start.45 = (f32[3,128,128]{2,1,0:T(8,128)S(1)}, f32[3,128,128]{2,1,0:T(8,128)S(1)}, u32[]{:S(2)}, u32[]{:S(2)}) collective-permute-start(f32[3,128,128]{2,1,0:T(8,128)S(1)} %collective-permute-done.44.refs_0_), channel_id=1, source_target_pairs={{0,8},{8,0},{16,24},{24,16},{1,9},{9,1},{17,25},{25,17},{2,10},{10... | collective-permute-start | bytes 589832 | tf_op jit(solution)/shard_map/cond/branch_6_fun/ppermute | solution.py:441
  52.1 12.0 %collective-permute-start.46 = (f32[3,128,128]{2,1,0:T(8,128)S(1)}, f32[3,128,128]{2,1,0:T(8,128)S(1)}, u32[]{:S(2)}, u32[]{:S(2)}) collective-permute-start(f32[3,128,128]{2,1,0:T(8,128)S(1)} %get-tuple-element.174), channel_id=1, source_target_pairs={{0,1},{1,0},{2,3},{3,2},{4,5},{5,4},{6,7},{7,6},{8,9},{9,8},{10,11... | collective-permute-start | bytes 589832 | tf_op jit(solution)/shard_map/cond/branch_6_fun/ppermute | solution.py:441
  56.4 7.7 %collective-permute-start.47 = (f32[3,128,128]{2,1,0:T(8,128)S(1)}, f32[3,128,128]{2,1,0:T(8,128)S(1)}, u32[]{:S(2)}, u32[]{:S(2)}) collective-permute-start(f32[3,128,128]{2,1,0:T(8,128)S(1)} %get-tuple-element.175), channel_id=1, source_target_pairs={{1,2},{3,4},{5,6},{2,1},{4,3},{6,5},{9,10},{11,12},{13,14},{10,9},... | collective-permute-start | bytes 589832 | tf_op jit(solution)/shard_map/cond/branch_6_fun/ppermute | solution.py:435
  66.5 1.1 %copy-start.5 = (f32[1,3,8,128,128]{4,3,2,1,0:T(8,128)}, f32[1,3,8,128,128]{4,3,2,1,0:T(8,128)S(1)}, u32[]{:S(2)}) copy-start(f32[1,3,8,128,128]{4,3,2,1,0:T(8,128)S(1)} %get-tuple-element.323) | copy-start | bytes 4718596
